TPU v7x, 32 devices: a whole 2x2x4 slice. The times are simulated.
32 devices in a mesh: grp: 4 (over y, core), ctx: 8 (over z, x).
Axes of the slice: x: 2, y: 2, z: 4, core: 2. Of those that a mesh axis runs over, the one named last changes fastest.
Arguments:
- queries: bfloat16 [64, 8192], P('grp'), may hold values from -250 to 250
- resident_key_cache: bfloat16 [64, 1024, 512], P('grp', 'ctx'), may hold values from -6 to 6
- resident_value_cache: bfloat16 [64, 1024, 512], P('grp', 'ctx'), may hold values from -6 to 6
- res_len: int32 [64], P('grp'), may hold values from 2 to 1024, as said below
- visual_page_pool: bfloat16 [4096, 2, 8, 512], P(('grp', 'ctx')), may hold values from -6 to 6
- recall_holder: int32 [8, 64, 16], P('ctx', 'grp'), may hold values from 0 to 31, all different within a row; in each aligned block of 16 rows (0 to 15, 16 to 31, ..., all dimensions but the last counted through in order) at most 16 rows name the same one
- recall_slot: int32 [8, 64, 16], P('ctx', 'grp'), may hold values from 0 to 127
- o_weight: bfloat16 [8192, 4096], P('ctx'), may hold values from -3 to 3
- residual: bfloat16 [64, 4096], P('grp'), may hold values from -60 to 60
- norm_gain: float32 [4096], replicated, may hold values from 0.5 to 1.5
- expert_ids: int32 [64, 8], P('grp'), may hold values from 0 to 31, all different within a row; in each aligned block of 16 rows (0 to 15, 16 to 31, ...) at most 4 rows name the same one
- expert_weights: float32 [64, 8], P('grp'), may hold values from 1 to 4
- w_gate: bfloat16 [32, 768, 4096], P(('grp', 'ctx')), may hold values from -0.09375 to 0.09375
- w_up: bfloat16 [32, 768, 4096], P(('grp', 'ctx')), may hold values from -0.09375 to 0.09375
- w_down: bfloat16 [32, 768, 4096], P(('grp', 'ctx')), may hold values from -0.21875 to 0.21875
Outputs:
- mixed: bfloat16 [64, 4096], P('grp', 'ctx')
Inputs may be any that keep to these rules, and one draw needn't show every extreme that they name: `res_len`: some request has length 1024 and some has length 2. `recall_holder`: the 16 holders of one request on one index of ctx differ; among the rows of one device (one index of ctx, the 16 requests of one group) no holder is named by more than 16 requests, and in some device's rows one holder by exactly 16. `expert_ids`: the 8 experts of a token differ; among the 16 tokens of one group no expert is named more than 4 times, and in some group one expert exactly 4 times.
All inputs are finite; a program needn't handle non-finite values.
Results may differ from a plain program's by a relative error of at most 0.025.
Values may be sent and summed in bfloat16 or wider, within the bound.
A program may use at most 128 MiB of HBM per device.

v0:
```python
import functools

import jax
import jax.numpy as jnp
from jax import lax
from jax.experimental import pallas as pl
from jax.experimental.pallas import tpu as pltpu
from jax.sharding import PartitionSpec as P

KEY_VALUE_HEADS = 4
HEAD_WIDTH = 128
EXP_GRP = 8
LANES = 128
CAPE = 4

VERY_NEGATIVE = -1e30
NORM_EPSILON = 1e-06
LOG2E = 1.4426950408889634
SCALE = HEAD_WIDTH ** (-0.5)

NT = (((1,), (1,)), ((), ()))
F32 = jnp.float32
BF16 = jnp.bfloat16


def wait_bytes(ref, sem):
    pltpu.make_async_copy(ref, ref, sem).wait()


def kernel(
    grp_count,
    ctx_count,
    page_tokens,
    q_hbm,
    kc_hbm,
    vc_hbm,
    rl_ref,
    pool_hbm,
    holder_ref,
    slot_ref,
    ow_hbm,
    res_ref,
    gain_ref,
    ids_ref,
    ew_ref,
    wg_hbm,
    wu_hbm,
    wd_hbm,
    out_ref,
    q_all,
    qt,
    kc,
    vc,
    pk,
    pv,
    ow,
    wg,
    wu,
    wd,
    turn,
    named,
    msg_ref,
    idx_recv,
    bias,
    o_res,
    l_res,
    o_send,
    o_recv,
    st_send,
    st_recv,
    mix_w,
    p_send,
    p_recv,
    x_send,
    x_recv,
    xs,
    y_send,
    y_recv,
    ys,
    local_sem,
    q_send_sem,
    q_recv_sem,
    send_sem,
    recv_sem,
):
    n = grp_count * ctx_count
    my_g = lax.axis_index("grp")
    my_c = lax.axis_index("ctx")
    me = my_g * ctx_count + my_c
    req = q_all.shape[1]
    heads = qt.shape[1]
    per_kv = heads // KEY_VALUE_HEADS
    heads_each = o_send.shape[2] // HEAD_WIDTH
    c_per_kv = per_kv // heads_each
    tokens = pk.shape[0] * page_tokens
    columns = p_send.shape[2]

    def dev(d):
        return (d // ctx_count, lax.rem(d, ctx_count))

    loads = [
        (q_hbm, q_all.at[my_g]),
        (kc_hbm, kc),
        (vc_hbm, vc),
        (pool_hbm.at[:, 0], pk),
        (pool_hbm.at[:, 1], pv),
        (ow_hbm, ow),
        (wg_hbm.at[0], wg),
        (wu_hbm.at[0], wu),
        (wd_hbm.at[0], wd),
    ]
    copies = [pltpu.make_async_copy(s, d, local_sem.at[i]) for i, (s, d) in enumerate(loads)]
    for copy in copies:
        copy.start()

    barrier = pltpu.get_barrier_semaphore()

    @pl.loop(1, n)
    def _(k):
        pl.semaphore_signal(
            barrier, inc=1, device_id=dev(lax.rem(me + k, n)), device_id_type=pl.DeviceIdType.MESH
        )

    lists = holder_ref.shape[1]
    for i, ref in enumerate((holder_ref, slot_ref)):
        turn[i] = jnp.zeros((LANES, LANES), F32)
        for r in range(3):
            turn[i, r * req : (r + 1) * req, 0:lists] = ref[...].astype(F32)
    holder_t = turn[0].T
    slot_t = turn[1].T
    holder_id = lax.broadcasted_iota(jnp.int32, (n, LANES), 0).astype(F32)
    table = jnp.zeros((n, LANES), F32)
    for j in range(lists):
        table = table + jnp.where(
            holder_t[j : j + 1, :] == holder_id, slot_t[j : j + 1, :] + 1.0, 0.0
        )
    named[...] = table

    @pl.loop(0, n)
    def _(d):
        msg_ref[d] = named[pl.ds(d, 1), :]

    pl.semaphore_wait(barrier, n - 1)

    def send(src, dst, s_sem, r_sem, target):
        pltpu.make_async_remote_copy(
            src_ref=src,
            dst_ref=dst,
            send_sem=s_sem,
            recv_sem=r_sem,
            device_id=target,
            device_id_type=pl.DeviceIdType.MESH,
        ).start()

    @pl.loop(1, n)
    def _(k):
        d = lax.rem(me + k, n)
        send(msg_ref.at[d], idx_recv.at[me], send_sem.at[0], recv_sem.at[0], dev(d))

    pairs = grp_count // 2
    pair_g = my_g + 1 - 2 * lax.rem(my_g, 2)
    for k in range(1, pairs):
        g = lax.rem(my_g + 2 * k, grp_count)
        send(q_hbm, q_all.at[my_g], q_send_sem, q_recv_sem.at[my_g], (g, my_c))
    send(q_hbm, q_all.at[my_g], q_send_sem, q_recv_sem.at[my_g], (pair_g, my_c))

    idx_recv[me] = msg_ref[me]

    copies[0].wait()
    for h in range(heads):
        qt[:, h, :] = q_all[my_g, :, h * HEAD_WIDTH : (h + 1) * HEAD_WIDTH].astype(F32)
    copies[1].wait()
    copies[2].wait()
    rows_here = kc.shape[1]

    def resident(t, carry):
        pos = my_c * rows_here + lax.broadcasted_iota(jnp.int32, (heads, rows_here), 1)
        ok = pos < rl_ref[t]
        s = jnp.concatenate(
            [
                lax.dot_general(
                    qt[t, k * per_kv : (k + 1) * per_kv, :].astype(BF16),
                    kc[t, :, k * HEAD_WIDTH : (k + 1) * HEAD_WIDTH],
                    NT,
                    preferred_element_type=F32,
                )
                for k in range(KEY_VALUE_HEADS)
            ],
            axis=0,
        )
        s = jnp.where(ok, s, VERY_NEGATIVE)
        m = jnp.max(s, axis=1, keepdims=True)
        p = jnp.exp2((s - m) * (SCALE * LOG2E))
        p = jnp.where(ok, p, 0.0)
        total = jnp.maximum(jnp.sum(p, axis=1, keepdims=True), 1e-30)
        pb = p.astype(BF16)
        o = jnp.concatenate(
            [
                jnp.dot(
                    pb[k * per_kv : (k + 1) * per_kv, :],
                    vc[t, :, k * HEAD_WIDTH : (k + 1) * HEAD_WIDTH],
                    preferred_element_type=F32,
                )
                for k in range(KEY_VALUE_HEADS)
            ],
            axis=0,
        )
        o_res[t] = o / total
        lse = m * (SCALE * LOG2E) + jnp.log(total) * LOG2E
        l_res[t] = jnp.broadcast_to(lse, (heads, LANES))
        return carry

    lax.fori_loop(0, req, resident, 0, unroll=4)

    wait_bytes(idx_recv.at[pl.ds(0, n - 1)], recv_sem.at[0])
    page_count = tokens // page_tokens
    lane = lax.broadcasted_iota(jnp.int32, (page_count, LANES), 1)
    page_id = (lax.broadcasted_iota(jnp.int32, (page_count, LANES), 0) + 1).astype(F32)
    spread = (
        lax.broadcasted_iota(jnp.int32, (tokens, page_count), 0) // page_tokens
        == lax.broadcasted_iota(jnp.int32, (tokens, page_count), 1)
    ).astype(F32).astype(BF16)

    @pl.loop(0, grp_count)
    def _(g):
        def add(c, count):
            row = idx_recv[g * ctx_count + c]
            return count + (jnp.broadcast_to(row, page_id.shape) == page_id).astype(F32)

        count = lax.fori_loop(0, ctx_count, add, jnp.zeros((page_count, LANES), F32))
        level = jnp.where(
            count > 0.0, jnp.log(jnp.maximum(count, 1.0)) * (1.0 / SCALE), VERY_NEGATIVE
        )
        hi = level.astype(BF16).astype(F32)
        rest = jnp.where(count > 0.0, level - hi, 0.0)
        mid = rest.astype(BF16).astype(F32)
        low = rest - mid
        part = jnp.where(lane < req, hi, jnp.where(lane < 2 * req, mid, low))
        part = jnp.where(lane < 3 * req, part, 0.0).astype(BF16)
        bias[g] = jnp.dot(spread, part, preferred_element_type=F32).astype(BF16)

    copies[3].wait()
    copies[4].wait()
    rows = per_kv * req
    row_t = lax.rem(lax.broadcasted_iota(jnp.int32, (rows, LANES), 0), req)
    row_lane = lax.broadcasted_iota(jnp.int32, (rows, LANES), 1)
    chooser = (
        ((lax.rem(row_lane, req) == row_t) & (row_lane < 3 * req)).astype(F32).astype(BF16)
    )
    st_lane = lax.broadcasted_iota(jnp.int32, (req, LANES), 1)

    def pool_part(g, own):
        def one(kv, carry):
            qk = jnp.concatenate(
                [
                    q_all[
                        g,
                        :,
                        pl.ds(pl.multiple_of((kv * per_kv + h) * HEAD_WIDTH, HEAD_WIDTH), HEAD_WIDTH),
                    ]
                    for h in range(per_kv)
                ],
                axis=0,
            )
            kv_cols = pl.ds(pl.multiple_of(kv * HEAD_WIDTH, HEAD_WIDTH), HEAD_WIDTH)
            qa = jnp.concatenate([qk, chooser], axis=1)
            ka = jnp.concatenate([pk[:, :, kv_cols].reshape(tokens, HEAD_WIDTH), bias[g]], axis=1)
            s = lax.dot_general(qa, ka, NT, preferred_element_type=F32)
            m = jnp.max(s, axis=1, keepdims=True)
            p = jnp.exp2((s - m) * (SCALE * LOG2E))
            total = jnp.sum(p, axis=1, keepdims=True)
            o = jnp.dot(
                p.astype(BF16),
                pv[:, :, kv_cols].reshape(tokens, HEAD_WIDTH),
                preferred_element_type=F32,
            ) / total
            lse = m * (SCALE * LOG2E) + jnp.log(total) * LOG2E
            for b in range(c_per_kv):
                block = g * ctx_count + kv * c_per_kv + b
                stat = jnp.zeros((req, LANES), F32)
                for j in range(heads_each):
                    h = b * heads_each + j
                    o_h = o[h * req : (h + 1) * req, :]
                    l_h = lse[h * req : (h + 1) * req, :]
                    if own:
                        o_r = o_res[:, kv * per_kv + h, :]
                        l_r = l_res[:, kv * per_kv + h, :]
                        l_b = jnp.broadcast_to(l_h, (req, LANES))
                        top = jnp.maximum(l_b, l_r)
                        w_p = jnp.exp2(l_b - top)
                        w_r = jnp.exp2(l_r - top)
                        o_h = (w_p * o_h + w_r * o_r) / (w_p + w_r)
                        l_h = top + jnp.log(w_p + w_r) * LOG2E
                    o_send[block, :, j * HEAD_WIDTH : (j + 1) * HEAD_WIDTH] = o_h.astype(BF16)
                    stat = jnp.where(st_lane == j, l_h, stat)
                st_send[block] = stat
            return carry

        lax.fori_loop(0, KEY_VALUE_HEADS, one, 0)

        @pl.loop(0, ctx_count)
        def _(k):
            d = g * ctx_count + lax.rem(my_c + k, ctx_count)

            @pl.when(d != me)
            def _():
                send(o_send.at[d], o_recv.at[me], send_sem.at[1], recv_sem.at[1], dev(d))
                send(st_send.at[d], st_recv.at[me], send_sem.at[2], recv_sem.at[2], dev(d))

    pool_part(my_g, True)
    o_recv[me] = o_send[me]
    st_recv[me] = st_send[me]

    @pl.loop(1, grp_count)
    def _(k):
        direct = (k >= 2) & (k < pairs + 1)
        g = jnp.where(
            direct,
            lax.rem(my_g + 2 * (k - 1), grp_count),
            lax.rem(pair_g + jnp.where(k == 1, 0, 2 * (k - pairs)), grp_count),
        )
        wait_bytes(q_all.at[g], q_recv_sem.at[g])

        @pl.when(direct)
        def _():
            send(q_all.at[g], q_all.at[g], q_send_sem, q_recv_sem.at[g], (pair_g, my_c))

        pool_part(g, False)

    wait_bytes(st_recv.at[pl.ds(0, n - 1)], recv_sem.at[2])
    top = lax.fori_loop(
        1, n, lambda i, a: jnp.maximum(a, st_recv[i]), st_recv[0]
    )

    def weigh(i, total):
        w = jnp.exp2(st_recv[i] - top)
        mix_w[i] = w
        return total + w

    total = lax.fori_loop(0, n, weigh, jnp.zeros((req, LANES), F32))
    inverse = 1.0 / total
    wait_bytes(o_recv.at[pl.ds(0, n - 1)], recv_sem.at[1])

    def join(i, acc):
        w = mix_w[i] * inverse
        return tuple(
            acc[j]
            + w[:, j : j + 1] * o_recv[i, :, j * HEAD_WIDTH : (j + 1) * HEAD_WIDTH].astype(F32)
            for j in range(heads_each)
        )

    acc = lax.fori_loop(
        0, n, join, tuple(jnp.zeros((req, HEAD_WIDTH), F32) for _ in range(heads_each))
    )
    attn = jnp.concatenate([a.astype(BF16) for a in acc], axis=1)

    copies[5].wait()

    @pl.loop(0, ctx_count)
    def _(k):
        c = lax.rem(my_c + k + 1, ctx_count)
        cols = pl.ds(pl.multiple_of(c * columns, columns), columns)
        p_send[c] = jnp.dot(attn, ow[:, cols], preferred_element_type=F32).astype(BF16)

        @pl.when(c != my_c)
        def _():
            send(p_send.at[c], p_recv.at[my_c], send_sem.at[3], recv_sem.at[3], (my_g, c))

    p_recv[my_c] = p_send[my_c]

    experts = grp_count * EXP_GRP
    places = experts * CAPE
    expert_id = lax.broadcasted_iota(jnp.int32, (experts, req), 0)
    taken = jnp.zeros((experts, req), F32)
    table = jnp.zeros((experts, req), F32)
    for k in range(ids_ref.shape[0]):
        match = ids_ref[k : k + 1, :] == expert_id
        taken = taken + jnp.where(match, 1.0, 0.0)
        table = table + jnp.where(match, ew_ref[k : k + 1, :], 0.0)
    before = (
        lax.broadcasted_iota(jnp.int32, (req, req), 0)
        < lax.broadcasted_iota(jnp.int32, (req, req), 1)
    ).astype(F32)
    exact = functools.partial(
        jnp.dot, precision=lax.Precision.HIGHEST, preferred_element_type=F32
    )
    order = exact(taken, before)
    repeat = (
        lax.broadcasted_iota(jnp.int32, (places, experts), 0) // CAPE
        == lax.broadcasted_iota(jnp.int32, (places, experts), 1)
    ).astype(F32)
    slot = lax.rem(lax.broadcasted_iota(jnp.int32, (places, req), 0), CAPE).astype(F32)
    picked = (exact(repeat, taken) > 0.5) & (jnp.abs(exact(repeat, order) - slot) < 0.5)
    picker = picked.astype(F32).astype(BF16)
    gates = jnp.where(picked, exact(repeat, table), 0.0)
    tables = []
    for f in range(0, places, LANES):
        turn[0] = jnp.zeros((LANES, LANES), F32)
        turn[0, :, 0:req] = gates[f : f + LANES, :]
        tables.append(turn[0].T[0:req, :])
    wait_bytes(p_recv.at[pl.ds(0, ctx_count - 1)], recv_sem.at[3])
    own_cols = pl.ds(pl.multiple_of(my_c * columns, columns), columns)
    hidden = lax.fori_loop(
        0, ctx_count, lambda c, a: a + p_recv[c].astype(F32), res_ref[:, own_cols].astype(F32)
    )
    outgoing = jnp.dot(picker, hidden.astype(BF16), preferred_element_type=F32)
    for e in range(experts):
        x_send[e] = outgoing[e * CAPE : (e + 1) * CAPE, :].astype(BF16)
    parts_count = ctx_count // EXP_GRP

    def expert_of(d):
        return (d // ctx_count) * EXP_GRP + lax.rem(d, ctx_count) // parts_count

    x_recv[me] = x_send[expert_of(me)]

    @pl.loop(1, n)
    def _(k):
        d = lax.rem(me + k, n)
        send(x_send.at[expert_of(d)], x_recv.at[me], send_sem.at[4], recv_sem.at[4], dev(d))

    for i in range(6, 9):
        copies[i].wait()
    wait_bytes(x_recv.at[pl.ds(0, n - 1)], recv_sem.at[4])

    @pl.loop(0, ctx_count)
    def _(c):
        cols = pl.ds(pl.multiple_of(c * columns, columns), columns)
        for g in range(grp_count):
            xs[g * CAPE : (g + 1) * CAPE, cols] = x_recv[g * ctx_count + c].astype(F32)

    x = xs[...]
    factor = lax.rsqrt(jnp.mean(x * x, axis=1, keepdims=True) + NORM_EPSILON)
    x = (x * factor * gain_ref[...]).astype(BF16)
    units = wg.shape[0]
    step = 256 if units % 256 == 0 else units
    acts = []
    for f in range(0, units, step):
        gate = lax.dot_general(x, wg[f : f + step, :], NT, preferred_element_type=F32)
        up = lax.dot_general(x, wu[f : f + step, :], NT, preferred_element_type=F32)
        acts.append((gate / (1.0 + jnp.exp(-gate)) * up).astype(BF16))
    act = jnp.concatenate(acts, axis=1)

    @pl.loop(0, ctx_count)
    def _(k):
        c = lax.rem(my_c + k + 1, ctx_count)
        cols = pl.ds(pl.multiple_of(c * columns, columns), columns)
        y = jnp.dot(act, wd[:, cols], preferred_element_type=F32)
        for g in range(grp_count):
            y_send[g * ctx_count + c] = y[g * CAPE : (g + 1) * CAPE, :].astype(BF16)

        @pl.loop(0, grp_count)
        def _(j):
            d = lax.rem(my_g + j + 1, grp_count) * ctx_count + c

            @pl.when(d != me)
            def _():
                send(y_send.at[d], y_recv.at[me], send_sem.at[5], recv_sem.at[5], dev(d))

    y_recv[me] = y_send[me]
    wait_bytes(y_recv.at[pl.ds(0, n - 1)], recv_sem.at[5])
    for e in range(experts):
        first = e * parts_count
        y = y_recv[first].astype(F32)
        for part in range(1, parts_count):
            y = y + y_recv[first + part].astype(F32)
        ys[e * CAPE : (e + 1) * CAPE, :] = y
    out = hidden
    for f, gates in enumerate(tables):
        out = out + exact(gates, ys[f * LANES : (f + 1) * LANES, :])
    out_ref[...] = out.astype(BF16)

    wait_bytes(idx_recv.at[pl.ds(0, n - 1)], send_sem.at[0])
    wait_bytes(q_all.at[pl.ds(0, grp_count - 1)], q_send_sem)
    wait_bytes(o_send.at[pl.ds(0, n - 1)], send_sem.at[1])
    wait_bytes(st_send.at[pl.ds(0, n - 1)], send_sem.at[2])
    wait_bytes(p_send.at[pl.ds(0, ctx_count - 1)], send_sem.at[3])
    wait_bytes(x_recv.at[pl.ds(0, n - 1)], send_sem.at[4])
    wait_bytes(y_send.at[pl.ds(0, n - 1)], send_sem.at[5])


def shards(
    queries,
    resident_key_cache,
    resident_value_cache,
    res_len,
    visual_page_pool,
    recall_holder,
    recall_slot,
    o_weight,
    residual,
    norm_gain,
    expert_ids,
    expert_weights,
    w_gate,
    w_up,
    w_down,
):
    ctx_count = lax.axis_size("ctx")
    grp_count = lax.axis_size("grp")
    n = ctx_count * grp_count
    req, q_width = queries.shape
    heads = q_width // HEAD_WIDTH
    own_width = o_weight.shape[0]
    pages, _, page_tokens, kv_width = visual_page_pool.shape
    tokens = pages * page_tokens
    width = residual.shape[1]
    columns = width // ctx_count
    units = w_gate.shape[1]
    rows_here = resident_key_cache.shape[1]

    smem = pl.BlockSpec(memory_space=pltpu.SMEM)
    vmem = pl.BlockSpec(memory_space=pltpu.VMEM)
    hbm = pl.BlockSpec(memory_space=pl.ANY)
    return pl.pallas_call(
        functools.partial(kernel, grp_count, ctx_count, page_tokens),
        out_shape=jax.ShapeDtypeStruct((req, columns), BF16),
        in_specs=[hbm, hbm, hbm, smem, hbm, vmem, vmem, hbm, vmem, vmem, vmem, vmem, hbm, hbm, hbm],
        out_specs=vmem,
        scratch_shapes=[
            pltpu.VMEM((grp_count, req, q_width), BF16),
            pltpu.VMEM((req, heads, HEAD_WIDTH), F32),
            pltpu.VMEM((req, rows_here, kv_width), BF16),
            pltpu.VMEM((req, rows_here, kv_width), BF16),
            pltpu.VMEM((pages, page_tokens, kv_width), BF16),
            pltpu.VMEM((pages, page_tokens, kv_width), BF16),
            pltpu.VMEM(o_weight.shape, BF16),
            pltpu.VMEM((units, width), BF16),
            pltpu.VMEM((units, width), BF16),
            pltpu.VMEM((units, width), BF16),
            pltpu.VMEM((2, LANES, LANES), F32),
            pltpu.VMEM((n, LANES), F32),
            pltpu.VMEM((n, 1, LANES), F32),
            pltpu.VMEM((n, 1, LANES), F32),
            pltpu.VMEM((grp_count, tokens, LANES), BF16),
            pltpu.VMEM((req, heads, HEAD_WIDTH), F32),
            pltpu.VMEM((req, heads, HEAD_WIDTH), F32),
            pltpu.VMEM((n, req, own_width), BF16),
            pltpu.VMEM((n, req, own_width), BF16),
            pltpu.VMEM((n, req, LANES), F32),
            pltpu.VMEM((n, req, LANES), F32),
            pltpu.VMEM((n, req, LANES), F32),
            pltpu.VMEM((ctx_count, req, columns), BF16),
            pltpu.VMEM((ctx_count, req, columns), BF16),
            pltpu.VMEM((grp_count * EXP_GRP, CAPE, columns), BF16),
            pltpu.VMEM((n, CAPE, columns), BF16),
            pltpu.VMEM((grp_count * CAPE, width), F32),
            pltpu.VMEM((n, CAPE, columns), BF16),
            pltpu.VMEM((n, CAPE, columns), BF16),
            pltpu.VMEM((grp_count * EXP_GRP * CAPE, columns), F32),
            pltpu.SemaphoreType.DMA((9,)),
            pltpu.SemaphoreType.DMA,
            pltpu.SemaphoreType.DMA((grp_count,)),
            pltpu.SemaphoreType.DMA((6,)),
            pltpu.SemaphoreType.DMA((6,)),
        ],
        compiler_params=pltpu.CompilerParams(
            collective_id=0, has_side_effects=True, vmem_limit_bytes=60 * 1024 * 1024
        ),
    )(
        queries,
        resident_key_cache,
        resident_value_cache,
        res_len,
        visual_page_pool,
        recall_holder[0],
        recall_slot[0],
        o_weight,
        residual,
        norm_gain.reshape(1, width),
        expert_ids.T,
        expert_weights.T,
        w_gate,
        w_up,
        w_down,
    )


def solution(mesh):
    placed = (
        P("grp", None),
        P("grp", "ctx", None),
        P("grp", "ctx", None),
        P("grp"),
        P(("grp", "ctx"), None, None, None),
        P("ctx", "grp", None),
        P("ctx", "grp", None),
        P("ctx", None),
        P("grp", None),
        P(),
        P("grp", None),
        P("grp", None),
        P(("grp", "ctx"), None, None),
        P(("grp", "ctx"), None, None),
        P(("grp", "ctx"), None, None),
    )
    return jax.shard_map(
        shards, mesh=mesh, in_specs=placed, out_specs=P("grp", "ctx"), check_vma=False
    )
```

profile of v0, /device:TPU:0, one launch (start us, length us, event | category | flops | bytes accessed | tf_op | source)
XLA Modules:
  0.0 74.0 jit_solution(13324872671442085544)
XLA Ops:
  0.0 72.6 %shard_map.145 = bf16[16,512]{1,0:T(8,128)(2,1)} custom-call(bf16[16,8192]{1,0:T(8,128)(2,1)} %q_hbm.1, bf16[16,128,512]{2,1,0:T(8,128)(2,1)} %kc_hbm.1, bf16[16,128,512]{2,1,0:T(8,128)(2,1)} %vc_hbm.1, s32[16]{0:T(128)} %rl_ref.1, bf16[128,2,8,512]{3,2,1,0:T(8,128)(2,1)} %pool_hbm.1, s32[16,16]{1,0:T(8,128)} %bitcast.6, s32[16,16]{1,0:T(8,128)} %bitcast.7, ...), custom_call_target="tpu_custom_call" | custom-call | tf_op jit(solution)/shard_map/pallas_call | solution.py:514
  72.6 1.3 %copy.17 = bf16[16,512]{1,0:T(8,128)(2,1)} copy(bf16[16,512]{1,0:T(8,128)(2,1)} %shard_map.145) | data formatting | bytes 32768
where the time goes:
time: 74.2 us; the launch traced here: 74 us
  Pallas kernels  72.6 us (98%)
  local copies, waits for them, and re-layouts  1.32 us (2%)
    pallas_call x1, Pallas kernels, shards(): pl.pallas_call(functools.partial(kernel, grp_count, ctx_count, page_token...  72.6 us

commit v1 on v0

--- a/solution.py
+++ b/solution.py
@@ -12,6 +12,8 @@
 EXP_GRP = 8
 LANES = 128
 CAPE = 4
+PARTS_APART = 32
+EARLY = 4
 
 VERY_NEGATIVE = -1e30
 NORM_EPSILON = 1e-06
@@ -64,10 +66,10 @@
     bias,
     o_res,
     l_res,
+    yo_send,
+    yo_recv,
     o_send,
     o_recv,
-    st_send,
-    st_recv,
     mix_w,
     p_send,
     p_recv,
@@ -80,6 +82,10 @@
     local_sem,
     q_send_sem,
     q_recv_sem,
+    pool_send_sem,
+    pool_recv_sem,
+    yo_send_sem,
+    yo_recv_sem,
     send_sem,
     recv_sem,
 ):
@@ -87,30 +93,46 @@
     my_g = lax.axis_index("grp")
     my_c = lax.axis_index("ctx")
     me = my_g * ctx_count + my_c
+    y_count = grp_count // 2
+    my_y = my_g // 2
+    my_core = lax.rem(my_g, 2)
+    pair = (my_g + 1 - 2 * my_core, my_c)
     req = q_all.shape[1]
     heads = qt.shape[1]
     per_kv = heads // KEY_VALUE_HEADS
-    heads_each = o_send.shape[2] // HEAD_WIDTH
+    own_width = o_send.shape[2] - LANES
+    heads_each = own_width // HEAD_WIDTH
     c_per_kv = per_kv // heads_each
-    tokens = pk.shape[0] * page_tokens
+    page_count = pk.shape[1]
+    tokens = page_count * page_tokens
     columns = p_send.shape[2]
+    same_core = y_count * ctx_count
+    mine = my_y * ctx_count + my_c
 
     def dev(d):
         return (d // ctx_count, lax.rem(d, ctx_count))
 
+    def far_first(k, count, at):
+        above, below = count - 1 - at, at
+        most, least = jnp.maximum(above, below), jnp.minimum(above, below)
+        lead = most - least
+        j = jnp.maximum(k - lead, 0)
+        side = jnp.where(above >= below, 1, -1) * (1 - 2 * lax.rem(j, 2))
+        return at + side * jnp.where(k < lead, most - k, least - j // 2)
+
     loads = [
-        (q_hbm, q_all.at[my_g]),
         (kc_hbm, kc),
         (vc_hbm, vc),
-        (pool_hbm.at[:, 0], pk),
-        (pool_hbm.at[:, 1], pv),
+        (q_hbm, q_all.at[my_y]),
+        (pool_hbm.at[:, 0], pk.at[my_core]),
+        (pool_hbm.at[:, 1], pv.at[my_core]),
         (ow_hbm, ow),
         (wg_hbm.at[0], wg),
         (wu_hbm.at[0], wu),
         (wd_hbm.at[0], wd),
     ]
     copies = [pltpu.make_async_copy(s, d, local_sem.at[i]) for i, (s, d) in enumerate(loads)]
-    for copy in copies:
+    for copy in copies[:5]:
         copy.start()
 
     barrier = pltpu.get_barrier_semaphore()
@@ -136,41 +158,12 @@
         )
     named[...] = table
 
-    @pl.loop(0, n)
-    def _(d):
-        msg_ref[d] = named[pl.ds(d, 1), :]
-
-    pl.semaphore_wait(barrier, n - 1)
-
-    def send(src, dst, s_sem, r_sem, target):
-        pltpu.make_async_remote_copy(
-            src_ref=src,
-            dst_ref=dst,
-            send_sem=s_sem,
-            recv_sem=r_sem,
-            device_id=target,
-            device_id_type=pl.DeviceIdType.MESH,
-        ).start()
-
-    @pl.loop(1, n)
-    def _(k):
-        d = lax.rem(me + k, n)
-        send(msg_ref.at[d], idx_recv.at[me], send_sem.at[0], recv_sem.at[0], dev(d))
-
-    pairs = grp_count // 2
-    pair_g = my_g + 1 - 2 * lax.rem(my_g, 2)
-    for k in range(1, pairs):
-        g = lax.rem(my_g + 2 * k, grp_count)
-        send(q_hbm, q_all.at[my_g], q_send_sem, q_recv_sem.at[my_g], (g, my_c))
-    send(q_hbm, q_all.at[my_g], q_send_sem, q_recv_sem.at[my_g], (pair_g, my_c))
-
-    idx_recv[me] = msg_ref[me]
-
-    copies[0].wait()
-    for h in range(heads):
-        qt[:, h, :] = q_all[my_g, :, h * HEAD_WIDTH : (h + 1) * HEAD_WIDTH].astype(F32)
-    copies[1].wait()
-    copies[2].wait()
+    @pl.loop(0, same_core)
+    def _(i):
+        first = (i // ctx_count) * 2 * ctx_count + lax.rem(i, ctx_count)
+        msg_ref[i, 0:1, :] = named[pl.ds(first, 1), :]
+        msg_ref[i, 1:2, :] = named[pl.ds(first + ctx_count, 1), :]
+
     rows_here = kc.shape[1]
 
     def resident(t, carry):
@@ -210,10 +203,56 @@
         l_res[t] = jnp.broadcast_to(lse, (heads, LANES))
         return carry
 
-    lax.fori_loop(0, req, resident, 0, unroll=4)
-
-    wait_bytes(idx_recv.at[pl.ds(0, n - 1)], recv_sem.at[0])
-    page_count = tokens // page_tokens
+    copies[0].wait()
+    copies[1].wait()
+    copies[2].wait()
+    for h in range(heads):
+        qt[:, h, :] = q_all[my_y, :, h * HEAD_WIDTH : (h + 1) * HEAD_WIDTH].astype(F32)
+    lax.fori_loop(0, EARLY, resident, 0, unroll=4)
+
+    pl.semaphore_wait(barrier, n - 1)
+
+    def send(src, dst, s_sem, r_sem, target):
+        pltpu.make_async_remote_copy(
+            src_ref=src,
+            dst_ref=dst,
+            send_sem=s_sem,
+            recv_sem=r_sem,
+            device_id=target,
+            device_id_type=pl.DeviceIdType.MESH,
+        ).start()
+
+    for i in range(2):
+        send(
+            pool_hbm.at[:, i],
+            (pk, pv)[i].at[my_core],
+            pool_send_sem.at[i],
+            pool_recv_sem.at[i],
+            pair,
+        )
+
+    @pl.loop(1, same_core)
+    def _(k):
+        i = lax.rem(mine + k, same_core)
+        send(
+            msg_ref.at[i],
+            idx_recv.at[mine],
+            send_sem.at[0],
+            recv_sem.at[0],
+            ((i // ctx_count) * 2 + my_core, lax.rem(i, ctx_count)),
+        )
+
+    for k in range(1, y_count):
+        y = lax.rem(my_y + k, y_count)
+        send(q_hbm, q_all.at[my_y], q_send_sem, q_recv_sem.at[my_y], (y * 2 + my_core, my_c))
+
+    for copy in copies[5:]:
+        copy.start()
+
+    idx_recv[mine] = msg_ref[mine]
+    lax.fori_loop(EARLY, req, resident, 0, unroll=4)
+
+    wait_bytes(idx_recv.at[pl.ds(0, same_core - 1)], recv_sem.at[0])
     lane = lax.broadcasted_iota(jnp.int32, (page_count, LANES), 1)
     page_id = (lax.broadcasted_iota(jnp.int32, (page_count, LANES), 0) + 1).astype(F32)
     spread = (
@@ -221,26 +260,31 @@
         == lax.broadcasted_iota(jnp.int32, (tokens, page_count), 1)
     ).astype(F32).astype(BF16)
 
-    @pl.loop(0, grp_count)
-    def _(g):
-        def add(c, count):
-            row = idx_recv[g * ctx_count + c]
-            return count + (jnp.broadcast_to(row, page_id.shape) == page_id).astype(F32)
-
-        count = lax.fori_loop(0, ctx_count, add, jnp.zeros((page_count, LANES), F32))
-        level = jnp.where(
-            count > 0.0, jnp.log(jnp.maximum(count, 1.0)) * (1.0 / SCALE), VERY_NEGATIVE
-        )
-        hi = level.astype(BF16).astype(F32)
-        rest = jnp.where(count > 0.0, level - hi, 0.0)
-        mid = rest.astype(BF16).astype(F32)
-        low = rest - mid
-        part = jnp.where(lane < req, hi, jnp.where(lane < 2 * req, mid, low))
-        part = jnp.where(lane < 3 * req, part, 0.0).astype(BF16)
-        bias[g] = jnp.dot(spread, part, preferred_element_type=F32).astype(BF16)
+    @pl.loop(0, y_count)
+    def _(y):
+        for core in range(2):
+            def add(c, count):
+                row = idx_recv[y * ctx_count + c, core : core + 1, :]
+                return count + (jnp.broadcast_to(row, page_id.shape) == page_id).astype(F32)
+
+            count = lax.fori_loop(0, ctx_count, add, jnp.zeros((page_count, LANES), F32), unroll=8)
+            level = jnp.where(
+                count > 0.0, jnp.log(jnp.maximum(count, 1.0)) * (1.0 / SCALE), VERY_NEGATIVE
+            )
+            hi = level.astype(BF16).astype(F32)
+            rest = jnp.where(count > 0.0, level - hi, 0.0)
+            mid = rest.astype(BF16).astype(F32)
+            low = rest - mid
+            part = jnp.where(lane < req, hi, jnp.where(lane < 2 * req, mid, low))
+            part = jnp.where(lane < 3 * req, part, 0.0).astype(BF16)
+            bias[y, core * tokens : (core + 1) * tokens, :] = jnp.dot(
+                spread, part, preferred_element_type=F32
+            ).astype(BF16)
 
     copies[3].wait()
     copies[4].wait()
+    wait_bytes(pk.at[0], pool_recv_sem.at[0])
+    wait_bytes(pv.at[0], pool_recv_sem.at[1])
     rows = per_kv * req
     row_t = lax.rem(lax.broadcasted_iota(jnp.int32, (rows, LANES), 0), req)
     row_lane = lax.broadcasted_iota(jnp.int32, (rows, LANES), 1)
@@ -249,97 +293,125 @@
     )
     st_lane = lax.broadcasted_iota(jnp.int32, (req, LANES), 1)
 
-    def pool_part(g, own):
-        def one(kv, carry):
-            qk = jnp.concatenate(
-                [
-                    q_all[
-                        g,
-                        :,
-                        pl.ds(pl.multiple_of((kv * per_kv + h) * HEAD_WIDTH, HEAD_WIDTH), HEAD_WIDTH),
-                    ]
-                    for h in range(per_kv)
-                ],
-                axis=0,
+    def encode(stat):
+        hi = stat.astype(BF16).astype(F32)
+        rest = stat - hi
+        mid = rest.astype(BF16).astype(F32)
+        low = rest - mid
+        return (hi + pltpu.roll(mid, PARTS_APART, 1) + pltpu.roll(low, 2 * PARTS_APART, 1)).astype(BF16)
+
+    def decode(block):
+        x = block.astype(F32)
+        return (
+            x + pltpu.roll(x, LANES - PARTS_APART, 1) + pltpu.roll(x, LANES - 2 * PARTS_APART, 1)
+        )
+
+    def pool_part(y, kv):
+        qk = jnp.concatenate(
+            [
+                q_all[
+                    y,
+                    :,
+                    pl.ds(pl.multiple_of((kv * per_kv + h) * HEAD_WIDTH, HEAD_WIDTH), HEAD_WIDTH),
+                ]
+                for h in range(per_kv)
+            ],
+            axis=0,
+        )
+        kv_cols = pl.ds(pl.multiple_of(kv * HEAD_WIDTH, HEAD_WIDTH), HEAD_WIDTH)
+        qa = jnp.concatenate([qk, chooser], axis=1)
+        ka = jnp.concatenate(
+            [pk[:, :, :, kv_cols].reshape(2 * tokens, HEAD_WIDTH), bias[y]], axis=1
+        )
+        s = lax.dot_general(qa, ka, NT, preferred_element_type=F32)
+        m = jnp.max(s, axis=1, keepdims=True)
+        p = jnp.exp2((s - m) * (SCALE * LOG2E)).astype(BF16)
+        va = jnp.concatenate(
+            [
+                pv[:, :, :, kv_cols].reshape(2 * tokens, HEAD_WIDTH),
+                jnp.ones((2 * tokens, LANES), BF16),
+            ],
+            axis=1,
+        )
+        o = jnp.dot(p, va, preferred_element_type=F32)
+        top = jnp.broadcast_to(m * (SCALE * LOG2E), (rows, LANES))
+        return o[:, :HEAD_WIDTH], o[:, HEAD_WIDTH:], top
+
+    def of_head(x, h):
+        return x[h * req : (h + 1) * req, :]
+
+    @pl.loop(1, y_count)
+    def _(k):
+        y = lax.rem(my_y + k, y_count)
+        wait_bytes(q_all.at[y], q_recv_sem.at[y])
+        for kv in range(KEY_VALUE_HEADS):
+            o, total, top = pool_part(y, kv)
+            o = o / total
+            lse = top + jnp.log(total) * LOG2E
+            stat = jnp.zeros((req, LANES), F32)
+            for h in range(per_kv):
+                yo_send[kv, y, :, h * HEAD_WIDTH : (h + 1) * HEAD_WIDTH] = of_head(o, h).astype(BF16)
+                stat = jnp.where(st_lane == h, of_head(lse, h), stat)
+            yo_send[kv, y, :, per_kv * HEAD_WIDTH :] = encode(stat)
+            send(
+                yo_send.at[kv, y],
+                yo_recv.at[kv, my_y],
+                yo_send_sem.at[kv],
+                yo_recv_sem.at[kv],
+                (y * 2 + my_core, my_c),
             )
-            kv_cols = pl.ds(pl.multiple_of(kv * HEAD_WIDTH, HEAD_WIDTH), HEAD_WIDTH)
-            qa = jnp.concatenate([qk, chooser], axis=1)
-            ka = jnp.concatenate([pk[:, :, kv_cols].reshape(tokens, HEAD_WIDTH), bias[g]], axis=1)
-            s = lax.dot_general(qa, ka, NT, preferred_element_type=F32)
-            m = jnp.max(s, axis=1, keepdims=True)
-            p = jnp.exp2((s - m) * (SCALE * LOG2E))
-            total = jnp.sum(p, axis=1, keepdims=True)
-            o = jnp.dot(
-                p.astype(BF16),
-                pv[:, :, kv_cols].reshape(tokens, HEAD_WIDTH),
-                preferred_element_type=F32,
-            ) / total
-            lse = m * (SCALE * LOG2E) + jnp.log(total) * LOG2E
-            for b in range(c_per_kv):
-                block = g * ctx_count + kv * c_per_kv + b
-                stat = jnp.zeros((req, LANES), F32)
-                for j in range(heads_each):
-                    h = b * heads_each + j
-                    o_h = o[h * req : (h + 1) * req, :]
-                    l_h = lse[h * req : (h + 1) * req, :]
-                    if own:
-                        o_r = o_res[:, kv * per_kv + h, :]
-                        l_r = l_res[:, kv * per_kv + h, :]
-                        l_b = jnp.broadcast_to(l_h, (req, LANES))
-                        top = jnp.maximum(l_b, l_r)
-                        w_p = jnp.exp2(l_b - top)
-                        w_r = jnp.exp2(l_r - top)
-                        o_h = (w_p * o_h + w_r * o_r) / (w_p + w_r)
-                        l_h = top + jnp.log(w_p + w_r) * LOG2E
-                    o_send[block, :, j * HEAD_WIDTH : (j + 1) * HEAD_WIDTH] = o_h.astype(BF16)
-                    stat = jnp.where(st_lane == j, l_h, stat)
-                st_send[block] = stat
-            return carry
-
-        lax.fori_loop(0, KEY_VALUE_HEADS, one, 0)
-
-        @pl.loop(0, ctx_count)
-        def _(k):
-            d = g * ctx_count + lax.rem(my_c + k, ctx_count)
-
-            @pl.when(d != me)
-            def _():
-                send(o_send.at[d], o_recv.at[me], send_sem.at[1], recv_sem.at[1], dev(d))
-                send(st_send.at[d], st_recv.at[me], send_sem.at[2], recv_sem.at[2], dev(d))
-
-    pool_part(my_g, True)
-    o_recv[me] = o_send[me]
-    st_recv[me] = st_send[me]
-
-    @pl.loop(1, grp_count)
-    def _(k):
-        direct = (k >= 2) & (k < pairs + 1)
-        g = jnp.where(
-            direct,
-            lax.rem(my_g + 2 * (k - 1), grp_count),
-            lax.rem(pair_g + jnp.where(k == 1, 0, 2 * (k - pairs)), grp_count),
-        )
-        wait_bytes(q_all.at[g], q_recv_sem.at[g])
-
-        @pl.when(direct)
-        def _():
-            send(q_all.at[g], q_all.at[g], q_send_sem, q_recv_sem.at[g], (pair_g, my_c))
-
-        pool_part(g, False)
-
-    wait_bytes(st_recv.at[pl.ds(0, n - 1)], recv_sem.at[2])
-    top = lax.fori_loop(
-        1, n, lambda i, a: jnp.maximum(a, st_recv[i]), st_recv[0]
-    )
+
+    my_kv = my_c // c_per_kv
+    for i in range(KEY_VALUE_HEADS):
+        kv = far_first(i, KEY_VALUE_HEADS, my_kv)
+        o, total, top = pool_part(my_y, kv)
+        wait_bytes(yo_recv.at[kv, pl.ds(0, y_count - 1)], yo_recv_sem.at[kv])
+        others = []
+        for k in range(1, y_count):
+            y = lax.rem(my_y + k, y_count)
+            others.append((y, decode(yo_recv[kv, y, :, per_kv * HEAD_WIDTH :])))
+        for b in range(c_per_kv):
+            c = kv * c_per_kv + b
+            stat = jnp.zeros((req, LANES), F32)
+            for j in range(heads_each):
+                h = b * heads_each + j
+                terms = [
+                    (of_head(top, h), of_head(total, h), of_head(o, h)),
+                    (l_res[:, kv * per_kv + h, :], None, o_res[:, kv * per_kv + h, :]),
+                ]
+                for y, l_y in others:
+                    o_y = yo_recv[kv, y, :, h * HEAD_WIDTH : (h + 1) * HEAD_WIDTH].astype(F32)
+                    terms.append((jnp.broadcast_to(l_y[:, h : h + 1], (req, LANES)), None, o_y))
+                best = functools.reduce(jnp.maximum, [t[0] for t in terms])
+                weights = [jnp.exp2(t[0] - best) for t in terms]
+                mass = sum(w if t[1] is None else w * t[1] for w, t in zip(weights, terms))
+                o_h = sum(w * t[2] for w, t in zip(weights, terms)) / mass
+                l_h = best + jnp.log(mass) * LOG2E
+                o_send[c, :, j * HEAD_WIDTH : (j + 1) * HEAD_WIDTH] = o_h.astype(BF16)
+                stat = jnp.where(st_lane == j, l_h, stat)
+            o_send[c, :, own_width:] = encode(stat)
+        last = i == KEY_VALUE_HEADS - 1
+        for b in range(1 if last else 0, c_per_kv):
+            c = kv * c_per_kv + (lax.rem(my_c + b, c_per_kv) if last else b)
+            send(o_send.at[c], o_recv.at[my_c], send_sem.at[1], recv_sem.at[1], (my_g, c))
+
+    o_recv[my_c] = o_send[my_c]
+    wait_bytes(o_recv.at[pl.ds(0, ctx_count - 1)], recv_sem.at[1])
+
+    def highest(i, top):
+        level = decode(o_recv[i, :, own_width:])
+        mix_w[i] = level
+        return jnp.maximum(top, level)
+
+    top = lax.fori_loop(0, ctx_count, highest, jnp.full((req, LANES), -3e38, F32), unroll=8)
 
     def weigh(i, total):
-        w = jnp.exp2(st_recv[i] - top)
+        w = jnp.exp2(mix_w[i] - top)
         mix_w[i] = w
         return total + w
 
-    total = lax.fori_loop(0, n, weigh, jnp.zeros((req, LANES), F32))
+    total = lax.fori_loop(0, ctx_count, weigh, jnp.zeros((req, LANES), F32), unroll=8)
     inverse = 1.0 / total
-    wait_bytes(o_recv.at[pl.ds(0, n - 1)], recv_sem.at[1])
 
     def join(i, acc):
         w = mix_w[i] * inverse
@@ -350,23 +422,27 @@
         )
 
     acc = lax.fori_loop(
-        0, n, join, tuple(jnp.zeros((req, HEAD_WIDTH), F32) for _ in range(heads_each))
+        0,
+        ctx_count,
+        join,
+        tuple(jnp.zeros((req, HEAD_WIDTH), F32) for _ in range(heads_each)),
+        unroll=8,
     )
     attn = jnp.concatenate([a.astype(BF16) for a in acc], axis=1)
 
     copies[5].wait()
 
-    @pl.loop(0, ctx_count)
+    def project(c):
+        cols = pl.ds(pl.multiple_of(c * columns, columns), columns)
+        return jnp.dot(attn, ow[:, cols], preferred_element_type=F32).astype(BF16)
+
+    @pl.loop(0, ctx_count - 1)
     def _(k):
-        c = lax.rem(my_c + k + 1, ctx_count)
-        cols = pl.ds(pl.multiple_of(c * columns, columns), columns)
-        p_send[c] = jnp.dot(attn, ow[:, cols], preferred_element_type=F32).astype(BF16)
-
-        @pl.when(c != my_c)
-        def _():
-            send(p_send.at[c], p_recv.at[my_c], send_sem.at[3], recv_sem.at[3], (my_g, c))
-
-    p_recv[my_c] = p_send[my_c]
+        c = far_first(k, ctx_count, my_c)
+        p_send[c] = project(c)
+        send(p_send.at[c], p_recv.at[my_c], send_sem.at[3], recv_sem.at[3], (my_g, c))
+
+    p_recv[my_c] = project(my_c)
 
     experts = grp_count * EXP_GRP
     places = experts * CAPE
@@ -469,10 +545,13 @@
         out = out + exact(gates, ys[f * LANES : (f + 1) * LANES, :])
     out_ref[...] = out.astype(BF16)
 
-    wait_bytes(idx_recv.at[pl.ds(0, n - 1)], send_sem.at[0])
-    wait_bytes(q_all.at[pl.ds(0, grp_count - 1)], q_send_sem)
-    wait_bytes(o_send.at[pl.ds(0, n - 1)], send_sem.at[1])
-    wait_bytes(st_send.at[pl.ds(0, n - 1)], send_sem.at[2])
+    wait_bytes(idx_recv.at[pl.ds(0, same_core - 1)], send_sem.at[0])
+    wait_bytes(q_all.at[pl.ds(0, y_count - 1)], q_send_sem)
+    wait_bytes(pk.at[0], pool_send_sem.at[0])
+    wait_bytes(pv.at[0], pool_send_sem.at[1])
+    for kv in range(KEY_VALUE_HEADS):
+        wait_bytes(yo_send.at[kv, pl.ds(0, y_count - 1)], yo_send_sem.at[kv])
+    wait_bytes(o_send.at[pl.ds(0, ctx_count - 1)], send_sem.at[1])
     wait_bytes(p_send.at[pl.ds(0, ctx_count - 1)], send_sem.at[3])
     wait_bytes(x_recv.at[pl.ds(0, n - 1)], send_sem.at[4])
     wait_bytes(y_send.at[pl.ds(0, n - 1)], send_sem.at[5])
@@ -500,6 +579,8 @@
     n = ctx_count * grp_count
     req, q_width = queries.shape
     heads = q_width // HEAD_WIDTH
+    y_count = grp_count // 2
+    kv_out = q_width // KEY_VALUE_HEADS
     own_width = o_weight.shape[0]
     pages, _, page_tokens, kv_width = visual_page_pool.shape
     tokens = pages * page_tokens
@@ -517,28 +598,28 @@
         in_specs=[hbm, hbm, hbm, smem, hbm, vmem, vmem, hbm, vmem, vmem, vmem, vmem, hbm, hbm, hbm],
         out_specs=vmem,
         scratch_shapes=[
-            pltpu.VMEM((grp_count, req, q_width), BF16),
+            pltpu.VMEM((y_count, req, q_width), BF16),
             pltpu.VMEM((req, heads, HEAD_WIDTH), F32),
             pltpu.VMEM((req, rows_here, kv_width), BF16),
             pltpu.VMEM((req, rows_here, kv_width), BF16),
-            pltpu.VMEM((pages, page_tokens, kv_width), BF16),
-            pltpu.VMEM((pages, page_tokens, kv_width), BF16),
+            pltpu.VMEM((2, pages, page_tokens, kv_width), BF16),
+            pltpu.VMEM((2, pages, page_tokens, kv_width), BF16),
             pltpu.VMEM(o_weight.shape, BF16),
             pltpu.VMEM((units, width), BF16),
             pltpu.VMEM((units, width), BF16),
             pltpu.VMEM((units, width), BF16),
             pltpu.VMEM((2, LANES, LANES), F32),
             pltpu.VMEM((n, LANES), F32),
-            pltpu.VMEM((n, 1, LANES), F32),
-            pltpu.VMEM((n, 1, LANES), F32),
-            pltpu.VMEM((grp_count, tokens, LANES), BF16),
+            pltpu.VMEM((y_count * ctx_count, 2, LANES), F32),
+            pltpu.VMEM((y_count * ctx_count, 2, LANES), F32),
+            pltpu.VMEM((y_count, 2 * tokens, LANES), BF16),
             pltpu.VMEM((req, heads, HEAD_WIDTH), F32),
             pltpu.VMEM((req, heads, HEAD_WIDTH), F32),
-            pltpu.VMEM((n, req, own_width), BF16),
-            pltpu.VMEM((n, req, own_width), BF16),
-            pltpu.VMEM((n, req, LANES), F32),
-            pltpu.VMEM((n, req, LANES), F32),
-            pltpu.VMEM((n, req, LANES), F32),
+            pltpu.VMEM((KEY_VALUE_HEADS, y_count, req, kv_out + LANES), BF16),
+            pltpu.VMEM((KEY_VALUE_HEADS, y_count, req, kv_out + LANES), BF16),
+            pltpu.VMEM((ctx_count, req, own_width + LANES), BF16),
+            pltpu.VMEM((ctx_count, req, own_width + LANES), BF16),
+            pltpu.VMEM((ctx_count, req, LANES), F32),
             pltpu.VMEM((ctx_count, req, columns), BF16),
             pltpu.VMEM((ctx_count, req, columns), BF16),
             pltpu.VMEM((grp_count * EXP_GRP, CAPE, columns), BF16),
@@ -549,7 +630,11 @@
             pltpu.VMEM((grp_count * EXP_GRP * CAPE, columns), F32),
             pltpu.SemaphoreType.DMA((9,)),
             pltpu.SemaphoreType.DMA,
-            pltpu.SemaphoreType.DMA((grp_count,)),
+            pltpu.SemaphoreType.DMA((y_count,)),
+            pltpu.SemaphoreType.DMA((2,)),
+            pltpu.SemaphoreType.DMA((2,)),
+            pltpu.SemaphoreType.DMA((KEY_VALUE_HEADS,)),
+            pltpu.SemaphoreType.DMA((KEY_VALUE_HEADS,)),
             pltpu.SemaphoreType.DMA((6,)),
             pltpu.SemaphoreType.DMA((6,)),
         ],

time: 74.2 us -> 56.4 us (0.76)
  Pallas kernels: 72.6 us -> 54.8 us
    pallas_call x1, Pallas kernels: 72.6 us -> 54.8 us  [shards(): pl.pallas_call(functools.partial(kernel, grp_count, ctx_count, page_token...]
where the time goes in v1:
time: 56.4 us; the launch traced here: 56.1 us
  Pallas kernels  54.8 us (97%)
  local copies, waits for them, and re-layouts  1.32 us (2%)
    pallas_call x1, Pallas kernels, shards(): pl.pallas_call(functools.partial(kernel, grp_count, ctx_count, page_token...  54.8 us
    unnamed x1, local copies, waits for them, and re-layouts  1.32 us

profile of v1, /device:TPU:0, one launch (start us, length us, event | category | flops | bytes accessed | tf_op | source)
XLA Modules:
  0.0 56.1 jit_solution(8982924993444952086)
XLA Ops:
  0.0 54.8 %shard_map.145 = bf16[16,512]{1,0:T(8,128)(2,1)} custom-call(bf16[16,8192]{1,0:T(8,128)(2,1)} %q_hbm.1, bf16[16,128,512]{2,1,0:T(8,128)(2,1)} %kc_hbm.1, bf16[16,128,512]{2,1,0:T(8,128)(2,1)} %vc_hbm.1, s32[16]{0:T(128)} %rl_ref.1, bf16[128,2,8,512]{3,2,1,0:T(8,128)(2,1)} %pool_hbm.1, s32[16,16]{1,0:T(8,128)} %bitcast.6, s32[16,16]{1,0:T(8,128)} %bitcast.7, ...), custom_call_target="tpu_custom_call" | custom-call | tf_op jit(solution)/shard_map/pallas_call | solution.py:595
  54.8 1.3 %copy.17 = bf16[16,512]{1,0:T(8,128)(2,1)} copy(bf16[16,512]{1,0:T(8,128)(2,1)} %shard_map.145) | data formatting | bytes 32768

commit v2 on v1

--- a/solution.py
+++ b/solution.py
@@ -75,7 +75,6 @@
     p_recv,
     x_send,
     x_recv,
-    xs,
     y_send,
     y_recv,
     ys,
@@ -86,6 +85,7 @@
     pool_recv_sem,
     yo_send_sem,
     yo_recv_sem,
+    x_recv_sem,
     send_sem,
     recv_sem,
 ):
@@ -100,6 +100,7 @@
     req = q_all.shape[1]
     heads = qt.shape[1]
     per_kv = heads // KEY_VALUE_HEADS
+    kv_out = per_kv * HEAD_WIDTH
     own_width = o_send.shape[2] - LANES
     heads_each = own_width // HEAD_WIDTH
     c_per_kv = per_kv // heads_each
@@ -120,10 +121,13 @@
         side = jnp.where(above >= below, 1, -1) * (1 - 2 * lax.rem(j, 2))
         return at + side * jnp.where(k < lead, most - k, least - j // 2)
 
+    early, late = pl.ds(0, EARLY), pl.ds(EARLY, req - EARLY)
     loads = [
-        (kc_hbm, kc),
-        (vc_hbm, vc),
         (q_hbm, q_all.at[my_y]),
+        (kc_hbm.at[early], kc.at[early]),
+        (vc_hbm.at[early], vc.at[early]),
+        (kc_hbm.at[late], kc.at[late]),
+        (vc_hbm.at[late], vc.at[late]),
         (pool_hbm.at[:, 0], pk.at[my_core]),
         (pool_hbm.at[:, 1], pv.at[my_core]),
         (ow_hbm, ow),
@@ -132,16 +136,23 @@
         (wd_hbm.at[0], wd),
     ]
     copies = [pltpu.make_async_copy(s, d, local_sem.at[i]) for i, (s, d) in enumerate(loads)]
-    for copy in copies[:5]:
+    for copy in copies[:7]:
         copy.start()
 
     barrier = pltpu.get_barrier_semaphore()
 
-    @pl.loop(1, n)
+    def greet(g, c):
+        pl.semaphore_signal(
+            barrier, inc=1, device_id=(g, c), device_id_type=pl.DeviceIdType.MESH
+        )
+
+    @pl.loop(0, ctx_count - 1)
     def _(k):
-        pl.semaphore_signal(
-            barrier, inc=1, device_id=dev(lax.rem(me + k, n)), device_id_type=pl.DeviceIdType.MESH
-        )
+        for g in range(grp_count):
+            greet(g, far_first(k, ctx_count, my_c))
+
+    for k in range(1, grp_count):
+        greet(lax.rem(my_g + k, grp_count), my_c)
 
     lists = holder_ref.shape[1]
     for i, ref in enumerate((holder_ref, slot_ref)):
@@ -204,10 +215,10 @@
         return carry
 
     copies[0].wait()
+    for h in range(heads):
+        qt[:, h, :] = q_all[my_y, :, h * HEAD_WIDTH : (h + 1) * HEAD_WIDTH].astype(F32)
     copies[1].wait()
     copies[2].wait()
-    for h in range(heads):
-        qt[:, h, :] = q_all[my_y, :, h * HEAD_WIDTH : (h + 1) * HEAD_WIDTH].astype(F32)
     lax.fori_loop(0, EARLY, resident, 0, unroll=4)
 
     pl.semaphore_wait(barrier, n - 1)
@@ -231,25 +242,42 @@
             pair,
         )
 
-    @pl.loop(1, same_core)
-    def _(k):
-        i = lax.rem(mine + k, same_core)
+    def send_lists(y, c):
         send(
-            msg_ref.at[i],
+            msg_ref.at[y * ctx_count + c],
             idx_recv.at[mine],
             send_sem.at[0],
             recv_sem.at[0],
-            ((i // ctx_count) * 2 + my_core, lax.rem(i, ctx_count)),
-        )
+            (y * 2 + my_core, c),
+        )
+
+    @pl.loop(0, ctx_count - 1)
+    def _(k):
+        for y in range(y_count):
+            send_lists(y, far_first(k, ctx_count, my_c))
+
+    for k in range(1, y_count):
+        send_lists(lax.rem(my_y + k, y_count), my_c)
 
     for k in range(1, y_count):
         y = lax.rem(my_y + k, y_count)
-        send(q_hbm, q_all.at[my_y], q_send_sem, q_recv_sem.at[my_y], (y * 2 + my_core, my_c))
-
-    for copy in copies[5:]:
+        for i in range(KEY_VALUE_HEADS):
+            kv = far_first(i, KEY_VALUE_HEADS, my_c // c_per_kv)
+            cols = pl.ds(pl.multiple_of(kv * kv_out, kv_out), kv_out)
+            send(
+                q_hbm.at[:, cols],
+                q_all.at[my_y, :, cols],
+                q_send_sem,
+                q_recv_sem.at[my_y, kv],
+                (y * 2 + my_core, my_c),
+            )
+
+    for copy in copies[7:]:
         copy.start()
 
     idx_recv[mine] = msg_ref[mine]
+    copies[3].wait()
+    copies[4].wait()
     lax.fori_loop(EARLY, req, resident, 0, unroll=4)
 
     wait_bytes(idx_recv.at[pl.ds(0, same_core - 1)], recv_sem.at[0])
@@ -281,8 +309,8 @@
                 spread, part, preferred_element_type=F32
             ).astype(BF16)
 
-    copies[3].wait()
-    copies[4].wait()
+    copies[5].wait()
+    copies[6].wait()
     wait_bytes(pk.at[0], pool_recv_sem.at[0])
     wait_bytes(pv.at[0], pool_recv_sem.at[1])
     rows = per_kv * req
@@ -306,7 +334,7 @@
             x + pltpu.roll(x, LANES - PARTS_APART, 1) + pltpu.roll(x, LANES - 2 * PARTS_APART, 1)
         )
 
-    def pool_part(y, kv):
+    def pool_scores(y, kv):
         qk = jnp.concatenate(
             [
                 q_all[
@@ -324,7 +352,10 @@
             [pk[:, :, :, kv_cols].reshape(2 * tokens, HEAD_WIDTH), bias[y]], axis=1
         )
         s = lax.dot_general(qa, ka, NT, preferred_element_type=F32)
-        m = jnp.max(s, axis=1, keepdims=True)
+        return s, jnp.max(s, axis=1, keepdims=True)
+
+    def pool_values(kv, s, m):
+        kv_cols = pl.ds(pl.multiple_of(kv * HEAD_WIDTH, HEAD_WIDTH), HEAD_WIDTH)
         p = jnp.exp2((s - m) * (SCALE * LOG2E)).astype(BF16)
         va = jnp.concatenate(
             [
@@ -337,63 +368,73 @@
         top = jnp.broadcast_to(m * (SCALE * LOG2E), (rows, LANES))
         return o[:, :HEAD_WIDTH], o[:, HEAD_WIDTH:], top
 
+    def pool_parts(y, kvs):
+        scores = [pool_scores(y, kv) for kv in kvs]
+        return [pool_values(kv, *x) for kv, x in zip(kvs, scores)]
+
     def of_head(x, h):
         return x[h * req : (h + 1) * req, :]
+
+    my_kv = my_c // c_per_kv
 
     @pl.loop(1, y_count)
     def _(k):
         y = lax.rem(my_y + k, y_count)
-        wait_bytes(q_all.at[y], q_recv_sem.at[y])
-        for kv in range(KEY_VALUE_HEADS):
-            o, total, top = pool_part(y, kv)
-            o = o / total
-            lse = top + jnp.log(total) * LOG2E
-            stat = jnp.zeros((req, LANES), F32)
-            for h in range(per_kv):
-                yo_send[kv, y, :, h * HEAD_WIDTH : (h + 1) * HEAD_WIDTH] = of_head(o, h).astype(BF16)
-                stat = jnp.where(st_lane == h, of_head(lse, h), stat)
-            yo_send[kv, y, :, per_kv * HEAD_WIDTH :] = encode(stat)
-            send(
-                yo_send.at[kv, y],
-                yo_recv.at[kv, my_y],
-                yo_send_sem.at[kv],
-                yo_recv_sem.at[kv],
-                (y * 2 + my_core, my_c),
-            )
-
-    my_kv = my_c // c_per_kv
-    for i in range(KEY_VALUE_HEADS):
-        kv = far_first(i, KEY_VALUE_HEADS, my_kv)
-        o, total, top = pool_part(my_y, kv)
-        wait_bytes(yo_recv.at[kv, pl.ds(0, y_count - 1)], yo_recv_sem.at[kv])
-        others = []
-        for k in range(1, y_count):
-            y = lax.rem(my_y + k, y_count)
-            others.append((y, decode(yo_recv[kv, y, :, per_kv * HEAD_WIDTH :])))
-        for b in range(c_per_kv):
-            c = kv * c_per_kv + b
-            stat = jnp.zeros((req, LANES), F32)
-            for j in range(heads_each):
-                h = b * heads_each + j
-                terms = [
-                    (of_head(top, h), of_head(total, h), of_head(o, h)),
-                    (l_res[:, kv * per_kv + h, :], None, o_res[:, kv * per_kv + h, :]),
-                ]
-                for y, l_y in others:
-                    o_y = yo_recv[kv, y, :, h * HEAD_WIDTH : (h + 1) * HEAD_WIDTH].astype(F32)
-                    terms.append((jnp.broadcast_to(l_y[:, h : h + 1], (req, LANES)), None, o_y))
-                best = functools.reduce(jnp.maximum, [t[0] for t in terms])
-                weights = [jnp.exp2(t[0] - best) for t in terms]
-                mass = sum(w if t[1] is None else w * t[1] for w, t in zip(weights, terms))
-                o_h = sum(w * t[2] for w, t in zip(weights, terms)) / mass
-                l_h = best + jnp.log(mass) * LOG2E
-                o_send[c, :, j * HEAD_WIDTH : (j + 1) * HEAD_WIDTH] = o_h.astype(BF16)
-                stat = jnp.where(st_lane == j, l_h, stat)
-            o_send[c, :, own_width:] = encode(stat)
-        last = i == KEY_VALUE_HEADS - 1
-        for b in range(1 if last else 0, c_per_kv):
-            c = kv * c_per_kv + (lax.rem(my_c + b, c_per_kv) if last else b)
-            send(o_send.at[c], o_recv.at[my_c], send_sem.at[1], recv_sem.at[1], (my_g, c))
+        for first in range(0, KEY_VALUE_HEADS, 2):
+            kvs = [far_first(first + i, KEY_VALUE_HEADS, my_kv) for i in range(2)]
+            for kv in kvs:
+                wait_bytes(q_all.at[y, :, pl.ds(0, kv_out)], q_recv_sem.at[y, kv])
+            for kv, (o, total, top) in zip(kvs, pool_parts(y, kvs)):
+                o = o / total
+                lse = top + jnp.log(total) * LOG2E
+                stat = jnp.zeros((req, LANES), F32)
+                for h in range(per_kv):
+                    yo_send[kv, y, :, h * HEAD_WIDTH : (h + 1) * HEAD_WIDTH] = of_head(o, h).astype(BF16)
+                    stat = jnp.where(st_lane == h, of_head(lse, h), stat)
+                yo_send[kv, y, :, kv_out:] = encode(stat)
+            for kv in kvs:
+                send(
+                    yo_send.at[kv, y],
+                    yo_recv.at[kv, my_y],
+                    yo_send_sem.at[kv],
+                    yo_recv_sem.at[kv],
+                    (y * 2 + my_core, my_c),
+                )
+
+    for first in range(0, KEY_VALUE_HEADS, 2):
+        kvs = [far_first(first + i, KEY_VALUE_HEADS, my_kv) for i in range(2)]
+        parts = pool_parts(my_y, kvs)
+        for kv in kvs:
+            wait_bytes(yo_recv.at[kv, pl.ds(0, y_count - 1)], yo_recv_sem.at[kv])
+        for i, (kv, (o, total, top)) in enumerate(zip(kvs, parts)):
+            others = []
+            for k in range(1, y_count):
+                y = lax.rem(my_y + k, y_count)
+                others.append((y, decode(yo_recv[kv, y, :, kv_out:])))
+            for b in range(c_per_kv):
+                c = kv * c_per_kv + b
+                stat = jnp.zeros((req, LANES), F32)
+                for j in range(heads_each):
+                    h = b * heads_each + j
+                    terms = [
+                        (of_head(top, h), of_head(total, h), of_head(o, h)),
+                        (l_res[:, kv * per_kv + h, :], None, o_res[:, kv * per_kv + h, :]),
+                    ]
+                    for y, l_y in others:
+                        o_y = yo_recv[kv, y, :, h * HEAD_WIDTH : (h + 1) * HEAD_WIDTH].astype(F32)
+                        terms.append((jnp.broadcast_to(l_y[:, h : h + 1], (req, LANES)), None, o_y))
+                    best = functools.reduce(jnp.maximum, [t[0] for t in terms])
+                    weights = [jnp.exp2(t[0] - best) for t in terms]
+                    mass = sum(w if t[1] is None else w * t[1] for w, t in zip(weights, terms))
+                    o_h = sum(w * t[2] for w, t in zip(weights, terms)) / mass
+                    l_h = best + jnp.log(mass) * LOG2E
+                    o_send[c, :, j * HEAD_WIDTH : (j + 1) * HEAD_WIDTH] = o_h.astype(BF16)
+                    stat = jnp.where(st_lane == j, l_h, stat)
+                o_send[c, :, own_width:] = encode(stat)
+            last = first + i == KEY_VALUE_HEADS - 1
+            for b in range(1 if last else 0, c_per_kv):
+                c = kv * c_per_kv + (lax.rem(my_c + b, c_per_kv) if last else b)
+                send(o_send.at[c], o_recv.at[my_c], send_sem.at[1], recv_sem.at[1], (my_g, c))
 
     o_recv[my_c] = o_send[my_c]
     wait_bytes(o_recv.at[pl.ds(0, ctx_count - 1)], recv_sem.at[1])
@@ -430,7 +471,7 @@
     )
     attn = jnp.concatenate([a.astype(BF16) for a in acc], axis=1)
 
-    copies[5].wait()
+    copies[7].wait()
 
     def project(c):
         cols = pl.ds(pl.multiple_of(c * columns, columns), columns)
@@ -487,51 +528,74 @@
     def expert_of(d):
         return (d // ctx_count) * EXP_GRP + lax.rem(d, ctx_count) // parts_count
 
-    x_recv[me] = x_send[expert_of(me)]
-
-    @pl.loop(1, n)
+    def dispatch(g, c):
+        send(
+            x_send.at[expert_of(g * ctx_count + c)],
+            x_recv.at[my_c, my_g],
+            send_sem.at[4],
+            x_recv_sem.at[my_c],
+            (g, c),
+        )
+
+    @pl.loop(0, ctx_count - 1)
     def _(k):
-        d = lax.rem(me + k, n)
-        send(x_send.at[expert_of(d)], x_recv.at[me], send_sem.at[4], recv_sem.at[4], dev(d))
-
-    for i in range(6, 9):
+        for g in range(grp_count):
+            dispatch(g, far_first(k, ctx_count, my_c))
+
+    for k in range(1, grp_count):
+        dispatch(lax.rem(my_g + k, grp_count), my_c)
+    x_recv[my_c, my_g] = x_send[expert_of(me)]
+
+    for i in range(8, 10):
         copies[i].wait()
-    wait_bytes(x_recv.at[pl.ds(0, n - 1)], recv_sem.at[4])
-
-    @pl.loop(0, ctx_count)
-    def _(c):
+    units = wg.shape[0]
+    width = wg.shape[1]
+    slots = grp_count * CAPE
+
+    def gate_up(c, carry):
+        squares, gate, up = carry
         cols = pl.ds(pl.multiple_of(c * columns, columns), columns)
-        for g in range(grp_count):
-            xs[g * CAPE : (g + 1) * CAPE, cols] = x_recv[g * ctx_count + c].astype(F32)
-
-    x = xs[...]
-    factor = lax.rsqrt(jnp.mean(x * x, axis=1, keepdims=True) + NORM_EPSILON)
-    x = (x * factor * gain_ref[...]).astype(BF16)
-    units = wg.shape[0]
-    step = 256 if units % 256 == 0 else units
-    acts = []
-    for f in range(0, units, step):
-        gate = lax.dot_general(x, wg[f : f + step, :], NT, preferred_element_type=F32)
-        up = lax.dot_general(x, wu[f : f + step, :], NT, preferred_element_type=F32)
-        acts.append((gate / (1.0 + jnp.exp(-gate)) * up).astype(BF16))
-    act = jnp.concatenate(acts, axis=1)
-
-    @pl.loop(0, ctx_count)
-    def _(k):
-        c = lax.rem(my_c + k + 1, ctx_count)
+        x = jnp.concatenate([x_recv[c, g].astype(F32) for g in range(grp_count)], axis=0)
+        squares = squares + jnp.sum(x * x, axis=1, keepdims=True)
+        x = (x * gain_ref[:, cols]).astype(BF16)
+        gate = gate + lax.dot_general(x, wg[:, cols], NT, preferred_element_type=F32)
+        up = up + lax.dot_general(x, wu[:, cols], NT, preferred_element_type=F32)
+        return squares, gate, up
+
+    def arrived(k, carry):
+        c = far_first(ctx_count - 1 - k, ctx_count, my_c)
+        wait_bytes(x_recv.at[c], x_recv_sem.at[c])
+        return gate_up(c, carry)
+
+    wait_bytes(x_recv.at[my_c, pl.ds(0, grp_count - 1)], x_recv_sem.at[my_c])
+    nothing = jnp.zeros((slots, units), F32)
+    carry = gate_up(my_c, (jnp.zeros((slots, 1), F32), nothing, nothing))
+    squares, gate, up = lax.fori_loop(1, ctx_count, arrived, carry)
+    factor = lax.rsqrt(squares * (1.0 / width) + NORM_EPSILON)
+    gate = gate * factor
+    up = up * factor
+    act = (gate / (1.0 + jnp.exp(-gate)) * up).astype(BF16)
+    copies[10].wait()
+
+    def down(c):
         cols = pl.ds(pl.multiple_of(c * columns, columns), columns)
         y = jnp.dot(act, wd[:, cols], preferred_element_type=F32)
         for g in range(grp_count):
             y_send[g * ctx_count + c] = y[g * CAPE : (g + 1) * CAPE, :].astype(BF16)
 
-        @pl.loop(0, grp_count)
-        def _(j):
-            d = lax.rem(my_g + j + 1, grp_count) * ctx_count + c
-
-            @pl.when(d != me)
-            def _():
-                send(y_send.at[d], y_recv.at[me], send_sem.at[5], recv_sem.at[5], dev(d))
-
+    def give_back(g, c):
+        send(y_send.at[g * ctx_count + c], y_recv.at[me], send_sem.at[5], recv_sem.at[5], (g, c))
+
+    @pl.loop(0, ctx_count - 1)
+    def _(k):
+        c = far_first(k, ctx_count, my_c)
+        down(c)
+        for g in range(grp_count):
+            give_back(g, c)
+
+    down(my_c)
+    for k in range(1, grp_count):
+        give_back(lax.rem(my_g + k, grp_count), my_c)
     y_recv[me] = y_send[me]
     wait_bytes(y_recv.at[pl.ds(0, n - 1)], recv_sem.at[5])
     for e in range(experts):
@@ -553,7 +617,7 @@
         wait_bytes(yo_send.at[kv, pl.ds(0, y_count - 1)], yo_send_sem.at[kv])
     wait_bytes(o_send.at[pl.ds(0, ctx_count - 1)], send_sem.at[1])
     wait_bytes(p_send.at[pl.ds(0, ctx_count - 1)], send_sem.at[3])
-    wait_bytes(x_recv.at[pl.ds(0, n - 1)], send_sem.at[4])
+    wait_bytes(y_recv.at[pl.ds(0, n - 1)], send_sem.at[4])
     wait_bytes(y_send.at[pl.ds(0, n - 1)], send_sem.at[5])
 
 
@@ -623,18 +687,18 @@
             pltpu.VMEM((ctx_count, req, columns), BF16),
             pltpu.VMEM((ctx_count, req, columns), BF16),
             pltpu.VMEM((grp_count * EXP_GRP, CAPE, columns), BF16),
-            pltpu.VMEM((n, CAPE, columns), BF16),
-            pltpu.VMEM((grp_count * CAPE, width), F32),
+            pltpu.VMEM((ctx_count, grp_count, CAPE, columns), BF16),
             pltpu.VMEM((n, CAPE, columns), BF16),
             pltpu.VMEM((n, CAPE, columns), BF16),
             pltpu.VMEM((grp_count * EXP_GRP * CAPE, columns), F32),
-            pltpu.SemaphoreType.DMA((9,)),
+            pltpu.SemaphoreType.DMA((11,)),
             pltpu.SemaphoreType.DMA,
-            pltpu.SemaphoreType.DMA((y_count,)),
+            pltpu.SemaphoreType.DMA((y_count, KEY_VALUE_HEADS)),
             pltpu.SemaphoreType.DMA((2,)),
             pltpu.SemaphoreType.DMA((2,)),
             pltpu.SemaphoreType.DMA((KEY_VALUE_HEADS,)),
             pltpu.SemaphoreType.DMA((KEY_VALUE_HEADS,)),
+            pltpu.SemaphoreType.DMA((ctx_count,)),
             pltpu.SemaphoreType.DMA((6,)),
             pltpu.SemaphoreType.DMA((6,)),
         ],

time: 56.4 us -> 48.6 us (0.86)
  Pallas kernels: 54.8 us -> 47 us
    pallas_call x1, Pallas kernels: 54.8 us -> 47 us  [shards(): pl.pallas_call(functools.partial(kernel, grp_count, ctx_count, page_token...]
where the time goes in v2:
time: 48.6 us; the launch traced here: 48.3 us
  Pallas kernels  47 us (97%)
  local copies, waits for them, and re-layouts  1.32 us (3%)
    pallas_call x1, Pallas kernels, shards(): pl.pallas_call(functools.partial(kernel, grp_count, ctx_count, page_token...  47 us
    unnamed x1, local copies, waits for them, and re-layouts  1.32 us

profile of v2, /device:TPU:0, one launch (start us, length us, event | category | flops | bytes accessed | tf_op | source)
XLA Modules:
  0.0 48.3 jit_solution(11907066913392886211)
XLA Ops:
  0.0 47.0 %shard_map.145 = bf16[16,512]{1,0:T(8,128)(2,1)} custom-call(bf16[16,8192]{1,0:T(8,128)(2,1)} %q_hbm.1, bf16[16,128,512]{2,1,0:T(8,128)(2,1)} %kc_hbm.1, bf16[16,128,512]{2,1,0:T(8,128)(2,1)} %vc_hbm.1, s32[16]{0:T(128)} %rl_ref.1, bf16[128,2,8,512]{3,2,1,0:T(8,128)(2,1)} %pool_hbm.1, s32[16,16]{1,0:T(8,128)} %bitcast.6, s32[16,16]{1,0:T(8,128)} %bitcast.7, ...), custom_call_target="tpu_custom_call" | custom-call | tf_op jit(solution)/shard_map/pallas_call | solution.py:659
  47.0 1.3 %copy.17 = bf16[16,512]{1,0:T(8,128)(2,1)} copy(bf16[16,512]{1,0:T(8,128)(2,1)} %shard_map.145) | data formatting | bytes 32768

commit v3 on v2

--- a/solution.py
+++ b/solution.py
@@ -36,19 +36,26 @@
     q_hbm,
     kc_hbm,
     vc_hbm,
+    rl_hbm,
+    pool_hbm,
+    holder_hbm,
+    slot_hbm,
+    ow_hbm,
+    res_hbm,
+    gain_hbm,
+    ids_hbm,
+    ew_hbm,
+    wg_hbm,
+    wu_hbm,
+    wd_hbm,
+    out_ref,
     rl_ref,
-    pool_hbm,
     holder_ref,
     slot_ref,
-    ow_hbm,
     res_ref,
     gain_ref,
     ids_ref,
     ew_ref,
-    wg_hbm,
-    wu_hbm,
-    wd_hbm,
-    out_ref,
     q_all,
     qt,
     kc,
@@ -79,6 +86,7 @@
     y_recv,
     ys,
     local_sem,
+    small_sem,
     q_send_sem,
     q_recv_sem,
     pool_send_sem,
@@ -136,7 +144,18 @@
         (wd_hbm.at[0], wd),
     ]
     copies = [pltpu.make_async_copy(s, d, local_sem.at[i]) for i, (s, d) in enumerate(loads)]
-    for copy in copies[:7]:
+    own_cols = pl.ds(pl.multiple_of(my_c * columns, columns), columns)
+    small_loads = [
+        (holder_hbm, holder_ref),
+        (slot_hbm, slot_ref),
+        (rl_hbm, rl_ref),
+        (ids_hbm, ids_ref),
+        (ew_hbm, ew_ref),
+        (res_hbm.at[:, own_cols], res_ref),
+        (gain_hbm, gain_ref),
+    ]
+    small = [pltpu.make_async_copy(s, d, small_sem.at[i]) for i, (s, d) in enumerate(small_loads)]
+    for copy in small[:2] + copies[:3] + small[2:] + copies[3:7]:
         copy.start()
 
     barrier = pltpu.get_barrier_semaphore()
@@ -154,6 +173,8 @@
     for k in range(1, grp_count):
         greet(lax.rem(my_g + k, grp_count), my_c)
 
+    small[0].wait()
+    small[1].wait()
     lists = holder_ref.shape[1]
     for i, ref in enumerate((holder_ref, slot_ref)):
         turn[i] = jnp.zeros((LANES, LANES), F32)
@@ -219,6 +240,7 @@
         qt[:, h, :] = q_all[my_y, :, h * HEAD_WIDTH : (h + 1) * HEAD_WIDTH].astype(F32)
     copies[1].wait()
     copies[2].wait()
+    small[2].wait()
     lax.fori_loop(0, EARLY, resident, 0, unroll=4)
 
     pl.semaphore_wait(barrier, n - 1)
@@ -233,6 +255,23 @@
             device_id_type=pl.DeviceIdType.MESH,
         ).start()
 
+    def send_lists(y, c):
+        send(
+            msg_ref.at[y * ctx_count + c],
+            idx_recv.at[mine],
+            send_sem.at[0],
+            recv_sem.at[0],
+            (y * 2 + my_core, c),
+        )
+
+    @pl.loop(0, ctx_count - 1)
+    def _(k):
+        for y in range(y_count):
+            send_lists(y, far_first(k, ctx_count, my_c))
+
+    for k in range(1, y_count):
+        send_lists(lax.rem(my_y + k, y_count), my_c)
+
     for i in range(2):
         send(
             pool_hbm.at[:, i],
@@ -241,23 +280,6 @@
             pool_recv_sem.at[i],
             pair,
         )
-
-    def send_lists(y, c):
-        send(
-            msg_ref.at[y * ctx_count + c],
-            idx_recv.at[mine],
-            send_sem.at[0],
-            recv_sem.at[0],
-            (y * 2 + my_core, c),
-        )
-
-    @pl.loop(0, ctx_count - 1)
-    def _(k):
-        for y in range(y_count):
-            send_lists(y, far_first(k, ctx_count, my_c))
-
-    for k in range(1, y_count):
-        send_lists(lax.rem(my_y + k, y_count), my_c)
 
     for k in range(1, y_count):
         y = lax.rem(my_y + k, y_count)
@@ -288,8 +310,7 @@
         == lax.broadcasted_iota(jnp.int32, (tokens, page_count), 1)
     ).astype(F32).astype(BF16)
 
-    @pl.loop(0, y_count)
-    def _(y):
+    def make_bias(y):
         for core in range(2):
             def add(c, count):
                 row = idx_recv[y * ctx_count + c, core : core + 1, :]
@@ -368,73 +389,81 @@
         top = jnp.broadcast_to(m * (SCALE * LOG2E), (rows, LANES))
         return o[:, :HEAD_WIDTH], o[:, HEAD_WIDTH:], top
 
-    def pool_parts(y, kvs):
-        scores = [pool_scores(y, kv) for kv in kvs]
-        return [pool_values(kv, *x) for kv, x in zip(kvs, scores)]
-
     def of_head(x, h):
         return x[h * req : (h + 1) * req, :]
 
     my_kv = my_c // c_per_kv
 
-    @pl.loop(1, y_count)
-    def _(k):
-        y = lax.rem(my_y + k, y_count)
-        for first in range(0, KEY_VALUE_HEADS, 2):
-            kvs = [far_first(first + i, KEY_VALUE_HEADS, my_kv) for i in range(2)]
-            for kv in kvs:
-                wait_bytes(q_all.at[y, :, pl.ds(0, kv_out)], q_recv_sem.at[y, kv])
-            for kv, (o, total, top) in zip(kvs, pool_parts(y, kvs)):
-                o = o / total
-                lse = top + jnp.log(total) * LOG2E
-                stat = jnp.zeros((req, LANES), F32)
-                for h in range(per_kv):
-                    yo_send[kv, y, :, h * HEAD_WIDTH : (h + 1) * HEAD_WIDTH] = of_head(o, h).astype(BF16)
-                    stat = jnp.where(st_lane == h, of_head(lse, h), stat)
-                yo_send[kv, y, :, kv_out:] = encode(stat)
-            for kv in kvs:
-                send(
-                    yo_send.at[kv, y],
-                    yo_recv.at[kv, my_y],
-                    yo_send_sem.at[kv],
-                    yo_recv_sem.at[kv],
-                    (y * 2 + my_core, my_c),
-                )
-
-    for first in range(0, KEY_VALUE_HEADS, 2):
-        kvs = [far_first(first + i, KEY_VALUE_HEADS, my_kv) for i in range(2)]
-        parts = pool_parts(my_y, kvs)
-        for kv in kvs:
-            wait_bytes(yo_recv.at[kv, pl.ds(0, y_count - 1)], yo_recv_sem.at[kv])
-        for i, (kv, (o, total, top)) in enumerate(zip(kvs, parts)):
-            others = []
-            for k in range(1, y_count):
-                y = lax.rem(my_y + k, y_count)
-                others.append((y, decode(yo_recv[kv, y, :, kv_out:])))
-            for b in range(c_per_kv):
-                c = kv * c_per_kv + b
-                stat = jnp.zeros((req, LANES), F32)
-                for j in range(heads_each):
-                    h = b * heads_each + j
-                    terms = [
-                        (of_head(top, h), of_head(total, h), of_head(o, h)),
-                        (l_res[:, kv * per_kv + h, :], None, o_res[:, kv * per_kv + h, :]),
-                    ]
-                    for y, l_y in others:
-                        o_y = yo_recv[kv, y, :, h * HEAD_WIDTH : (h + 1) * HEAD_WIDTH].astype(F32)
-                        terms.append((jnp.broadcast_to(l_y[:, h : h + 1], (req, LANES)), None, o_y))
-                    best = functools.reduce(jnp.maximum, [t[0] for t in terms])
-                    weights = [jnp.exp2(t[0] - best) for t in terms]
-                    mass = sum(w if t[1] is None else w * t[1] for w, t in zip(weights, terms))
-                    o_h = sum(w * t[2] for w, t in zip(weights, terms)) / mass
-                    l_h = best + jnp.log(mass) * LOG2E
-                    o_send[c, :, j * HEAD_WIDTH : (j + 1) * HEAD_WIDTH] = o_h.astype(BF16)
-                    stat = jnp.where(st_lane == j, l_h, stat)
-                o_send[c, :, own_width:] = encode(stat)
-            last = first + i == KEY_VALUE_HEADS - 1
-            for b in range(1 if last else 0, c_per_kv):
-                c = kv * c_per_kv + (lax.rem(my_c + b, c_per_kv) if last else b)
-                send(o_send.at[c], o_recv.at[my_c], send_sem.at[1], recv_sem.at[1], (my_g, c))
+    def finish_other(y, kv, o, total, top):
+        o = o / total
+        lse = top + jnp.log(total) * LOG2E
+        stat = jnp.zeros((req, LANES), F32)
+        for h in range(per_kv):
+            yo_send[kv, y, :, h * HEAD_WIDTH : (h + 1) * HEAD_WIDTH] = of_head(o, h).astype(BF16)
+            stat = jnp.where(st_lane == h, of_head(lse, h), stat)
+        yo_send[kv, y, :, kv_out:] = encode(stat)
+        send(
+            yo_send.at[kv, y],
+            yo_recv.at[kv, my_y],
+            yo_send_sem.at[kv],
+            yo_recv_sem.at[kv],
+            (y * 2 + my_core, my_c),
+        )
+
+    def finish_own(kv, o, total, top, last):
+        wait_bytes(yo_recv.at[kv, pl.ds(0, y_count - 1)], yo_recv_sem.at[kv])
+        others = []
+        for k in range(1, y_count):
+            y = lax.rem(my_y + k, y_count)
+            others.append((y, decode(yo_recv[kv, y, :, kv_out:])))
+        for b in range(c_per_kv):
+            c = kv * c_per_kv + b
+            stat = jnp.zeros((req, LANES), F32)
+            for j in range(heads_each):
+                h = b * heads_each + j
+                terms = [
+                    (of_head(top, h), of_head(total, h), of_head(o, h)),
+                    (l_res[:, kv * per_kv + h, :], None, o_res[:, kv * per_kv + h, :]),
+                ]
+                for y, l_y in others:
+                    o_y = yo_recv[kv, y, :, h * HEAD_WIDTH : (h + 1) * HEAD_WIDTH].astype(F32)
+                    terms.append((jnp.broadcast_to(l_y[:, h : h + 1], (req, LANES)), None, o_y))
+                best = functools.reduce(jnp.maximum, [t[0] for t in terms])
+                weights = [jnp.exp2(t[0] - best) for t in terms]
+                mass = sum(w if t[1] is None else w * t[1] for w, t in zip(weights, terms))
+                o_h = sum(w * t[2] for w, t in zip(weights, terms)) / mass
+                l_h = best + jnp.log(mass) * LOG2E
+                o_send[c, :, j * HEAD_WIDTH : (j + 1) * HEAD_WIDTH] = o_h.astype(BF16)
+                stat = jnp.where(st_lane == j, l_h, stat)
+            o_send[c, :, own_width:] = encode(stat)
+        for b in range(1 if last else 0, c_per_kv):
+            c = kv * c_per_kv + (lax.rem(my_c + b, c_per_kv) if last else b)
+            send(o_send.at[c], o_recv.at[my_c], send_sem.at[1], recv_sem.at[1], (my_g, c))
+
+    units = [(k, i) for k in (*range(1, y_count), 0) for i in range(KEY_VALUE_HEADS)]
+    places = [
+        (lax.rem(my_y + k, y_count), far_first(i, KEY_VALUE_HEADS, my_kv)) for k, i in units
+    ]
+
+    def scores_of(u):
+        y, kv = places[u]
+        if units[u][0]:
+            wait_bytes(q_all.at[y, :, pl.ds(0, kv_out)], q_recv_sem.at[y, kv])
+        return pool_scores(y, kv)
+
+    make_bias(places[0][0])
+    scores = scores_of(0)
+    for k in (*range(2, y_count), 0):
+        make_bias(lax.rem(my_y + k, y_count))
+    for u, (k, i) in enumerate(units):
+        y, kv = places[u]
+        following = scores_of(u + 1) if u + 1 < len(units) else None
+        part = pool_values(kv, *scores)
+        scores = following
+        if k:
+            finish_other(y, kv, *part)
+        else:
+            finish_own(kv, *part, i == KEY_VALUE_HEADS - 1)
 
     o_recv[my_c] = o_send[my_c]
     wait_bytes(o_recv.at[pl.ds(0, ctx_count - 1)], recv_sem.at[1])
@@ -488,6 +517,8 @@
     experts = grp_count * EXP_GRP
     places = experts * CAPE
     expert_id = lax.broadcasted_iota(jnp.int32, (experts, req), 0)
+    for copy in small[3:]:
+        copy.wait()
     taken = jnp.zeros((experts, req), F32)
     table = jnp.zeros((experts, req), F32)
     for k in range(ids_ref.shape[0]):
@@ -516,9 +547,8 @@
         turn[0, :, 0:req] = gates[f : f + LANES, :]
         tables.append(turn[0].T[0:req, :])
     wait_bytes(p_recv.at[pl.ds(0, ctx_count - 1)], recv_sem.at[3])
-    own_cols = pl.ds(pl.multiple_of(my_c * columns, columns), columns)
     hidden = lax.fori_loop(
-        0, ctx_count, lambda c, a: a + p_recv[c].astype(F32), res_ref[:, own_cols].astype(F32)
+        0, ctx_count, lambda c, a: a + p_recv[c].astype(F32), res_ref[...].astype(F32)
     )
     outgoing = jnp.dot(picker, hidden.astype(BF16), preferred_element_type=F32)
     for e in range(experts):
@@ -653,15 +683,21 @@
     units = w_gate.shape[1]
     rows_here = resident_key_cache.shape[1]
 
-    smem = pl.BlockSpec(memory_space=pltpu.SMEM)
     vmem = pl.BlockSpec(memory_space=pltpu.VMEM)
     hbm = pl.BlockSpec(memory_space=pl.ANY)
     return pl.pallas_call(
         functools.partial(kernel, grp_count, ctx_count, page_tokens),
-        out_shape=jax.ShapeDtypeStruct((req, columns), BF16),
-        in_specs=[hbm, hbm, hbm, smem, hbm, vmem, vmem, hbm, vmem, vmem, vmem, vmem, hbm, hbm, hbm],
+        out_shape=pltpu.VMEM((req, columns), BF16),
+        in_specs=[hbm] * 15,
         out_specs=vmem,
         scratch_shapes=[
+            pltpu.SMEM(res_len.shape, jnp.int32),
+            pltpu.VMEM(recall_holder.shape[1:], jnp.int32),
+            pltpu.VMEM(recall_slot.shape[1:], jnp.int32),
+            pltpu.VMEM((req, columns), BF16),
+            pltpu.VMEM((1, width), F32),
+            pltpu.VMEM(expert_ids.shape[::-1], jnp.int32),
+            pltpu.VMEM(expert_weights.shape[::-1], F32),
             pltpu.VMEM((y_count, req, q_width), BF16),
             pltpu.VMEM((req, heads, HEAD_WIDTH), F32),
             pltpu.VMEM((req, rows_here, kv_width), BF16),
@@ -692,6 +728,7 @@
             pltpu.VMEM((n, CAPE, columns), BF16),
             pltpu.VMEM((grp_count * EXP_GRP * CAPE, columns), F32),
             pltpu.SemaphoreType.DMA((11,)),
+            pltpu.SemaphoreType.DMA((7,)),
             pltpu.SemaphoreType.DMA,
             pltpu.SemaphoreType.DMA((y_count, KEY_VALUE_HEADS)),
             pltpu.SemaphoreType.DMA((2,)),

time: 48.6 us -> 45.9 us (0.944)
  Pallas kernels: 47 us -> 45.1 us
  local copies, waits for them, and re-layouts: 1.32 us -> 0.61 us
    pallas_call x1, Pallas kernels: 47 us -> 45.1 us  [shards(): pl.pallas_call(functools.partial(kernel, grp_count, ctx_count, page_token...]
    unnamed x1, local copies, waits for them, and re-layouts: 1.32 us -> 0.61 us
where the time goes in v3:
time: 45.9 us; the launch traced here: 45.7 us
  Pallas kernels  45.1 us (98%)
  local copies, waits for them, and re-layouts  0.61 us (1%)
    pallas_call x1, Pallas kernels, shards(): pl.pallas_call(functools.partial(kernel, grp_count, ctx_count, page_token...  45.1 us

profile of v3, /device:TPU:0, one launch (start us, length us, event | category | flops | bytes accessed | tf_op | source)
XLA Modules:
  0.0 45.7 jit_solution(11295939995760239411)
XLA Ops:
  0.0 45.1 %shard_map.145 = bf16[16,512]{1,0:T(8,128)(2,1)S(1)} custom-call(bf16[16,8192]{1,0:T(8,128)(2,1)} %q_hbm.1, bf16[16,128,512]{2,1,0:T(8,128)(2,1)} %kc_hbm.1, bf16[16,128,512]{2,1,0:T(8,128)(2,1)} %vc_hbm.1, s32[16]{0:T(128)} %rl_hbm.1, bf16[128,2,8,512]{3,2,1,0:T(8,128)(2,1)} %pool_hbm.1, s32[16,16]{1,0:T(8,128)} %bitcast.6, s32[16,16]{1,0:T(8,128)} %bitcast.7, ...), custom_call_target="tpu_custom_call" | custom-call | tf_op jit(solution)/shard_map/pallas_call | solution.py:688
  45.1 0.6 %copy.17 = bf16[16,512]{1,0:T(8,128)(2,1)} copy(bf16[16,512]{1,0:T(8,128)(2,1)S(1)} %shard_map.145) | data formatting | bytes 32768

commit v4 on v3

--- a/solution.py
+++ b/solution.py
@@ -155,7 +155,7 @@
         (gain_hbm, gain_ref),
     ]
     small = [pltpu.make_async_copy(s, d, small_sem.at[i]) for i, (s, d) in enumerate(small_loads)]
-    for copy in small[:2] + copies[:3] + small[2:] + copies[3:7]:
+    for copy in small[:2] + copies[:3] + small[2:3]:
         copy.start()
 
     barrier = pltpu.get_barrier_semaphore()
@@ -172,6 +172,8 @@
 
     for k in range(1, grp_count):
         greet(lax.rem(my_g + k, grp_count), my_c)
+    for copy in copies[3:7] + small[3:]:
+        copy.start()
 
     small[0].wait()
     small[1].wait()
@@ -584,23 +586,34 @@
 
     def gate_up(c, carry):
         squares, gate, up = carry
-        cols = pl.ds(pl.multiple_of(c * columns, columns), columns)
-        x = jnp.concatenate([x_recv[c, g].astype(F32) for g in range(grp_count)], axis=0)
+        cols = pl.ds(pl.multiple_of(c * columns, 2 * columns), 2 * columns)
+        x = jnp.concatenate(
+            [
+                jnp.concatenate([x_recv[c + i, g].astype(F32) for g in range(grp_count)], axis=0)
+                for i in range(2)
+            ],
+            axis=1,
+        )
         squares = squares + jnp.sum(x * x, axis=1, keepdims=True)
         x = (x * gain_ref[:, cols]).astype(BF16)
         gate = gate + lax.dot_general(x, wg[:, cols], NT, preferred_element_type=F32)
         up = up + lax.dot_general(x, wu[:, cols], NT, preferred_element_type=F32)
         return squares, gate, up
 
+    half = my_c // 2
+
     def arrived(k, carry):
-        c = far_first(ctx_count - 1 - k, ctx_count, my_c)
-        wait_bytes(x_recv.at[c], x_recv_sem.at[c])
+        c = 2 * far_first(ctx_count // 2 - 1 - k, ctx_count // 2, half)
+        for i in range(2):
+            wait_bytes(x_recv.at[c + i], x_recv_sem.at[c + i])
         return gate_up(c, carry)
 
     wait_bytes(x_recv.at[my_c, pl.ds(0, grp_count - 1)], x_recv_sem.at[my_c])
+    beside = my_c + 1 - 2 * lax.rem(my_c, 2)
+    wait_bytes(x_recv.at[beside], x_recv_sem.at[beside])
     nothing = jnp.zeros((slots, units), F32)
-    carry = gate_up(my_c, (jnp.zeros((slots, 1), F32), nothing, nothing))
-    squares, gate, up = lax.fori_loop(1, ctx_count, arrived, carry)
+    carry = gate_up(2 * half, (jnp.zeros((slots, 1), F32), nothing, nothing))
+    squares, gate, up = lax.fori_loop(1, ctx_count // 2, arrived, carry)
     factor = lax.rsqrt(squares * (1.0 / width) + NORM_EPSILON)
     gate = gate * factor
     up = up * factor

time: 45.9 us -> 45.7 us (level)
  no operation moved by 1% of the time
where the time goes in v4:
time: 45.7 us; the launch traced here: 45.5 us
  Pallas kernels  44.9 us (98%)
  local copies, waits for them, and re-layouts  0.61 us (1%)
    pallas_call x1, Pallas kernels, shards(): pl.pallas_call(functools.partial(kernel, grp_count, ctx_count, page_token...  44.9 us

profile of v4, /device:TPU:0, one launch (start us, length us, event | category | flops | bytes accessed | tf_op | source)
XLA Modules:
  0.0 45.5 jit_solution(7781248001236927497)
XLA Ops:
  0.0 44.9 %shard_map.145 = bf16[16,512]{1,0:T(8,128)(2,1)S(1)} custom-call(bf16[16,8192]{1,0:T(8,128)(2,1)} %q_hbm.1, bf16[16,128,512]{2,1,0:T(8,128)(2,1)} %kc_hbm.1, bf16[16,128,512]{2,1,0:T(8,128)(2,1)} %vc_hbm.1, s32[16]{0:T(128)} %rl_hbm.1, bf16[128,2,8,512]{3,2,1,0:T(8,128)(2,1)} %pool_hbm.1, s32[16,16]{1,0:T(8,128)} %bitcast.6, s32[16,16]{1,0:T(8,128)} %bitcast.7, ...), custom_call_target="tpu_custom_call" | custom-call | tf_op jit(solution)/shard_map/pallas_call | solution.py:701
  44.9 0.6 %copy.17 = bf16[16,512]{1,0:T(8,128)(2,1)} copy(bf16[16,512]{1,0:T(8,128)(2,1)S(1)} %shard_map.145) | data formatting | bytes 32768
